TPU v7x, 32 devices: a whole 2x2x4 slice. The times are simulated.
32 devices in a mesh: dp: 16 (over z, y, core), tensor: 2 (over x).
Axes of the slice: x: 2, y: 2, z: 4, core: 2. Of those that a mesh axis runs over, the one named last changes fastest.
Arguments:
- inputs: bfloat16 [4096, 1024], P('dp'), may hold values from -6 to 6
- qkv_weight: bfloat16 [2, 3, 1024, 1024], P(None, None, None, 'tensor'), may hold values from -0.1875 to 0.1875
- conv_taps: bfloat16 [2, 3, 4, 1024], P(None, None, None, 'tensor'), may hold values from -3 to 3
- beta_weight: bfloat16 [2, 1024, 8], P(None, None, 'tensor'), may hold values from -0.1875 to 0.1875
- out_gain: bfloat16 [2, 128], replicated, may hold values from 0.5 to 1.5
- out_weight: bfloat16 [2, 1024, 1024], P(None, 'tensor'), may hold values from -0.1875 to 0.1875
- norm_gain: bfloat16 [2, 2, 1024], replicated, may hold values from 0.5 to 1.5
- gate_up_weight: bfloat16 [2, 2, 1024, 2816], P(None, None, None, 'tensor'), may hold values from -0.1875 to 0.1875
- down_weight: bfloat16 [2, 2816, 1024], P(None, 'tensor'), may hold values from -0.109375 to 0.109375
- cotangent: bfloat16 [4096, 1024], P('dp'), may hold values from -6 to 6
Outputs:
- outputs: bfloat16 [4096, 1024], P('dp')
- input_grad: bfloat16 [4096, 1024], P('dp')
- grad_qkv: float32 [2, 3, 1024, 1024], P(None, None, None, 'tensor')
- grad_conv: float32 [2, 3, 4, 1024], P(None, None, None, 'tensor')
- grad_beta: float32 [2, 1024, 8], P(None, None, 'tensor')
- grad_out_gain: float32 [2, 128], replicated
- grad_out: float32 [2, 1024, 1024], P(None, 'tensor')
- grad_norm: float32 [2, 2, 1024], replicated
- grad_gate_up: float32 [2, 2, 1024, 2816], P(None, None, None, 'tensor')
- grad_down: float32 [2, 2816, 1024], P(None, 'tensor')
All inputs are finite; a program needn't handle non-finite values.
Results may differ from a plain program's by a relative error of at most 0.033.
Values may be sent and summed in bfloat16 or wider, within the bound.
A program may use at most 384 MiB of HBM per device.

v0:
```python
import math

import jax
import jax.numpy as jnp
from jax import lax
from jax.sharding import PartitionSpec as P

DK = 128
KCONV = 4
SPAN = 64
LAYERS = 2


HIGHEST = lax.Precision.HIGHEST


def rms_norm(source, gain):
    return source * lax.rsqrt(jnp.mean(source * source, axis=-1, keepdims=True) + 1e-05) * gain


def head_norm(source, gain):
    return source * lax.rsqrt(jnp.mean(source * source, axis=-1, keepdims=True) + 0.01) * gain


def unit_heads(source):
    return source * lax.rsqrt(jnp.sum(source * source, axis=-1, keepdims=True) + 0.001)


def prepare(project, taps, logits):
    length = project.shape[1]
    padded = jnp.pad(project, ((0, 0), (KCONV - 1, 0), (0, 0)))
    conv_sum = taps[:, 0, None, :] * padded[:, 0:length, :]
    for offset in range(1, KCONV):
        conv_sum = conv_sum + taps[:, offset, None, :] * padded[:, offset : offset + length, :]
    active = jax.nn.silu(conv_sum)
    per_head = active.reshape(3, length, -1, DK)
    return (unit_heads(per_head[0]), unit_heads(per_head[1]), per_head[2], jax.nn.sigmoid(logits))


def delta_rule(query_vec, key_vec, value_vec, beta_gate):
    length, head_count, head_size = query_vec.shape
    num_blocks = length // SPAN

    def blocked(source):
        return source.reshape(num_blocks, SPAN, head_count, -1).transpose(0, 2, 1, 3)

    beta_blocks = beta_gate.reshape(num_blocks, SPAN, head_count).transpose(0, 2, 1)
    strict = jnp.tril(jnp.ones((SPAN, SPAN), jnp.float32), -1)
    inclusive = jnp.tril(jnp.ones((SPAN, SPAN), jnp.float32))
    identity = jnp.eye(SPAN, dtype=jnp.float32)

    def block_step(memory, block):
        query_blk, key_blk, value_blk, beta_blk = block
        key_gram = jnp.einsum("hid,hjd->hij", key_blk, key_blk, precision=HIGHEST)
        unit_lower = identity + strict * (beta_blk[:, :, None] * key_gram)
        right_side = jnp.concatenate([key_blk, value_blk], axis=-1) * beta_blk[:, :, None]
        solved = lax.linalg.triangular_solve(
            unit_lower, right_side, left_side=True, lower=True, unit_diagonal=True
        )
        key_mix = solved[..., :head_size]
        value_mix = solved[..., head_size:]
        new_values = value_mix - jnp.einsum("hcd,hde->hce", key_mix, memory, precision=HIGHEST)
        scores = jnp.einsum("hid,hjd->hij", query_blk, key_blk, precision=HIGHEST) * inclusive
        result = jnp.einsum("hid,hde->hie", query_blk, memory, precision=HIGHEST)
        result = result + jnp.einsum("hij,hje->hie", scores, new_values, precision=HIGHEST)
        memory = memory + jnp.einsum("hjd,hje->hde", key_blk, new_values, precision=HIGHEST)
        return (memory, result)

    start_state = jnp.zeros((head_count, head_size, head_size), jnp.float32)
    _, results = lax.scan(
        block_step,
        start_state,
        (blocked(query_vec), blocked(key_vec), blocked(value_vec), beta_blocks),
    )
    return results.transpose(0, 2, 1, 3).reshape(length, head_count, head_size)


def gated_unit(gate_up):
    return jax.nn.silu(gate_up[0]) * gate_up[1]


def rounded_copy(source):
    return lax.optimization_barrier(source.astype(jnp.bfloat16)).astype(jnp.float32)


def rms_back(hidden, gain, grad_normed):
    scale = lax.rsqrt(jnp.mean(hidden * hidden, axis=-1, keepdims=True) + 1e-05)
    weighted = gain * grad_normed
    inner_mean = jnp.mean(hidden * weighted, axis=-1, keepdims=True)
    grad_hidden = scale * weighted - hidden * (scale * scale * scale) * inner_mean
    return (grad_hidden, grad_normed * hidden * scale)


def own_rows(full):
    count = full.shape[0] // lax.axis_size("tensor")
    return lax.dynamic_slice_in_dim(full, lax.axis_index("tensor") * count, count, 0)


def branch_total(partial_value):
    return lax.psum(partial_value.astype(jnp.bfloat16), "tensor").astype(jnp.float32)


def grad_total(partial_value):
    return lax.psum(partial_value.astype(jnp.bfloat16), "tensor").astype(jnp.float32)


def flatten_all(tables):
    return jnp.concatenate([table.reshape(-1) for table in tables])


def unflatten_all(flat, shapes):
    pieces = []
    offset = 0
    for shape in shapes:
        count = math.prod(shape)
        pieces.append(flat[offset : offset + count].reshape(shape))
        offset = offset + count
    return pieces


def body(
    inputs,
    qkv_weight,
    conv_taps,
    beta_weight,
    out_gain,
    out_weight,
    norm_gain,
    gate_up_weight,
    down_weight,
    cotangent,
):
    f32 = jnp.float32
    bf16 = jnp.bfloat16
    residual = inputs.astype(f32)
    kept = []
    for level in range(LAYERS):
        gains = norm_gain[level].astype(f32)
        normed = rms_norm(residual, gains[0]).astype(bf16)
        length = normed.shape[0]
        project = jnp.einsum("td,sdc->stc", normed, qkv_weight[level], preferred_element_type=f32)
        logits = jnp.dot(normed, beta_weight[level], preferred_element_type=f32)
        prepared, prep_back = jax.vjp(prepare, project, conv_taps[level].astype(f32), logits)
        query_vec, key_vec, value_vec, beta_gate = prepared
        mixer_out, delta_back = jax.vjp(
            delta_rule,
            rounded_copy(query_vec),
            rounded_copy(key_vec),
            rounded_copy(value_vec),
            beta_gate,
        )
        normed_heads, norm_back = jax.vjp(head_norm, mixer_out, out_gain[level].astype(f32))
        heads_out = normed_heads.astype(bf16).reshape(length, -1)
        hidden = residual + branch_total(
            jnp.dot(heads_out, out_weight[level], preferred_element_type=f32)
        )
        normed_two = rms_norm(hidden, gains[1]).astype(bf16)
        gate_up = jnp.einsum(
            "td,sdf->stf", normed_two, gate_up_weight[level], preferred_element_type=f32
        )
        inner_full, gate_back = jax.vjp(gated_unit, gate_up)
        inner_act = inner_full.astype(bf16)
        kept.append(
            (
                residual,
                gains,
                normed,
                heads_out,
                hidden,
                normed_two,
                inner_act,
                prep_back,
                delta_back,
                norm_back,
                gate_back,
                mixer_out.shape,
            )
        )
        residual = hidden + branch_total(
            jnp.dot(inner_act, down_weight[level], preferred_element_type=f32)
        )
    outputs = residual.astype(bf16)
    grad_res = cotangent.astype(f32)
    gain_list = [None] * LAYERS
    head_gain_list = [None] * LAYERS
    flat_list = [None] * LAYERS
    shapes = None
    for level in reversed(range(LAYERS)):
        (
            layer_in,
            gains,
            normed,
            heads_out,
            hidden,
            normed_two,
            inner_act,
            prep_back,
            delta_back,
            norm_back,
            gate_back,
            mixer_shape,
        ) = kept[level]
        grad_f = grad_res.astype(bf16)
        grad_inner = jnp.dot(grad_f, down_weight[level].T, preferred_element_type=f32)
        grad_down_l = jnp.dot(inner_act.T, grad_f, preferred_element_type=f32)
        grad_gu = gate_back(grad_inner)[0].astype(bf16)
        grad_gate_up_l = jnp.einsum("td,stf->sdf", normed_two, grad_gu, preferred_element_type=f32)
        grad_two = grad_total(
            jnp.einsum("stf,sdf->td", grad_gu, gate_up_weight[level], preferred_element_type=f32)
        )
        grad_hidden, gain_rows_two = rms_back(hidden, gains[1], grad_two)
        grad_res = grad_res + grad_hidden
        grad_m = grad_res.astype(bf16)
        grad_out_l = jnp.dot(heads_out.T, grad_m, preferred_element_type=f32)
        grad_heads = jnp.dot(grad_m, out_weight[level].T, preferred_element_type=f32).reshape(
            mixer_shape
        )
        grad_mix, grad_head_gain = norm_back(grad_heads)
        grad_query, grad_key, grad_value, grad_gate = delta_back(grad_mix)
        grad_proj, grad_conv_l, grad_logit = prep_back(
            (grad_query, grad_key, grad_value, grad_gate)
        )
        proj_low = grad_proj.astype(bf16)
        logit_low = grad_logit.astype(bf16)
        grad_qkv_l = jnp.einsum("td,stc->sdc", normed, proj_low, preferred_element_type=f32)
        grad_beta_l = jnp.dot(normed.T, logit_low, preferred_element_type=f32)
        grad_one_part = jnp.einsum(
            "stc,sdc->td", proj_low, qkv_weight[level], preferred_element_type=f32
        )
        grad_one_part = grad_one_part + jnp.dot(
            logit_low, beta_weight[level].T, preferred_element_type=f32
        )
        grad_one = grad_total(grad_one_part)
        grad_input, gain_rows_one = rms_back(layer_in, gains[0], grad_one)
        grad_res = grad_res + grad_input
        sum_one = jnp.sum(own_rows(gain_rows_one), axis=0)
        sum_two = jnp.sum(own_rows(gain_rows_two), axis=0)
        gain_list[level] = jnp.stack([sum_one, sum_two])
        head_gain_list[level] = grad_head_gain
        tables = (grad_qkv_l, grad_conv_l, grad_beta_l, grad_out_l, grad_gate_up_l, grad_down_l)
        shapes = [table.shape for table in tables]
        flat = flatten_all(tables)
        flat_list[level] = flat
    input_grad = grad_res.astype(bf16)
    joined = jnp.concatenate(flat_list)
    shard = lax.psum_scatter(
        joined.astype(jnp.bfloat16), "dp", scatter_dimension=0, tiled=True
    ).astype(jnp.float32)
    joined = lax.all_gather(shard.astype(jnp.bfloat16), "dp", axis=0, tiled=True).astype(
        shard.dtype
    )
    piece_len = flat_list[0].shape[0]
    summed_flat = [joined[level * piece_len : (level + 1) * piece_len] for level in range(LAYERS)]
    per_level = [unflatten_all(summed_flat[level], shapes) for level in range(LAYERS)]
    grad_norm, grad_out_gain = lax.psum(
        (jnp.stack(gain_list), jnp.stack(head_gain_list)), ("dp", "tensor")
    )
    grad_qkv = jnp.stack([pieces[0] for pieces in per_level])
    grad_conv = jnp.stack([pieces[1] for pieces in per_level])
    grad_beta = jnp.stack([pieces[2] for pieces in per_level])
    grad_out = jnp.stack([pieces[3] for pieces in per_level])
    grad_gate_up = jnp.stack([pieces[4] for pieces in per_level])
    grad_down = jnp.stack([pieces[5] for pieces in per_level])
    return (
        outputs,
        input_grad,
        grad_qkv,
        grad_conv,
        grad_beta,
        grad_out_gain,
        grad_out,
        grad_norm,
        grad_gate_up,
        grad_down,
    )


def solution(mesh):
    in_specs = (
        P("dp", None),
        P(None, None, None, "tensor"),
        P(None, None, None, "tensor"),
        P(None, None, "tensor"),
        P(),
        P(None, "tensor", None),
        P(),
        P(None, None, None, "tensor"),
        P(None, "tensor", None),
        P("dp", None),
    )
    out_specs = (
        P("dp", None),
        P("dp", None),
        P(None, None, None, "tensor"),
        P(None, None, None, "tensor"),
        P(None, None, "tensor"),
        P(),
        P(None, "tensor", None),
        P(),
        P(None, None, None, "tensor"),
        P(None, "tensor", None),
    )
    return jax.shard_map(body, mesh=mesh, in_specs=in_specs, out_specs=out_specs, check_vma=False)
```

profile of v0, /device:TPU:0, one launch (start us, length us, event | category | flops | bytes accessed | tf_op | source)
XLA Modules:
  0.0 1942.2 jit_solution(13018082781293137139)
XLA Ops:
  31.6 120.9 %while.114 = (s32[]{:T(128)}, f32[4,128,128]{2,1,0:T(8,128)S(1)}, f32[4,4,64,128]{3,2,1,0:T(8,128)S(1)}, f32[4,4,64,64]{3,2,1,0:T(8,128)}, f32[4,4,64,1]{2,1,3,0...) while((s32[]{:T(128)}, f32[4,128,128]{2,1,0:T(8,128)S(1)}, ...), condition=%wide.region_4.6_spmd.clone, body=%wide.region_3.5_spmd.clone.sunk | while | flops 277598272 | bytes 6640105 | solution.py:70
  37.1 19.7 %custom-call.28 = f32[4,1,64,64]{2,3,1,0:T(8,128)S(1)} custom-call(f32[4,1,64,64]{3,2,1,0:T(8,128)S(1)} %add_bitcast_fusion.8), custom_call_target="InvertDiagBlocksLowerTriangular" | custom-call | tf_op jit(solution)/shard_map/jvp()/while/body/eval_jaxpr/triangular_solve/custom-call.1 | solution.py:57
  67.3 19.7 %custom-call.28 = f32[4,1,64,64]{2,3,1,0:T(8,128)S(1)} custom-call(f32[4,1,64,64]{3,2,1,0:T(8,128)S(1)} %add_bitcast_fusion.8), custom_call_target="InvertDiagBlocksLowerTriangular" | custom-call | tf_op jit(solution)/shard_map/jvp()/while/body/eval_jaxpr/triangular_solve/custom-call.1 | solution.py:57
  97.5 19.7 %custom-call.28 = f32[4,1,64,64]{2,3,1,0:T(8,128)S(1)} custom-call(f32[4,1,64,64]{3,2,1,0:T(8,128)S(1)} %add_bitcast_fusion.8), custom_call_target="InvertDiagBlocksLowerTriangular" | custom-call | tf_op jit(solution)/shard_map/jvp()/while/body/eval_jaxpr/triangular_solve/custom-call.1 | solution.py:57
  127.8 19.7 %custom-call.28 = f32[4,1,64,64]{2,3,1,0:T(8,128)S(1)} custom-call(f32[4,1,64,64]{3,2,1,0:T(8,128)S(1)} %add_bitcast_fusion.8), custom_call_target="InvertDiagBlocksLowerTriangular" | custom-call | tf_op jit(solution)/shard_map/jvp()/while/body/eval_jaxpr/triangular_solve/custom-call.1 | solution.py:57
  156.4 31.4 %all-reduce.44.cloned.1.call-done = bf16[256,1024]{1,0:T(8,128)(2,1)} async-done(((bf16[256,1024]{1,0:T(8,128)(2,1)}), bf16[256,1024]{1,0:T(8,128)(2,1)}) %all-reduce.44.cloned.1.call-update) | async-done | bytes 524304 | tf_op jit(solution)/shard_map/psum | solution.py:100
  202.7 24.7 %all-reduce.46.cloned.1.call-done = bf16[256,1024]{1,0:T(8,128)(2,1)} async-done(((bf16[256,1024]{1,0:T(8,128)(2,1)}), bf16[256,1024]{1,0:T(8,128)(2,1)}) %all-reduce.46.cloned.1.call-update) | async-done | bytes 524304 | tf_op jit(solution)/shard_map/psum | solution.py:100
  252.1 131.6 %while.115 = (s32[]{:T(128)}, f32[4,128,128]{2,1,0:T(8,128)S(1)}, f32[4,4,64,128]{3,2,1,0:T(8,128)}, f32[4,4,64,64]{3,2,1,0:T(8,128)}, f32[4,4,64,1]{2,1,3,0:T(4...) while((s32[]{:T(128)}, f32[4,128,128]{2,1,0:T(8,128)S(1)}, ...), condition=%wide.region_13.15_spmd.clone, body=%wide.region_12.14_spmd.clone.sunk | while | flops 277598272 | bytes 6641129 | solution.py:70
  259.7 19.7 %custom-call.29 = f32[4,1,64,64]{2,3,1,0:T(8,128)S(1)} custom-call(f32[4,1,64,64]{3,2,1,0:T(8,128)S(1)} %add_bitcast_fusion.9), custom_call_target="InvertDiagBlocksLowerTriangular" | custom-call | tf_op jit(solution)/shard_map/jvp()/while/body/eval_jaxpr/triangular_solve/custom-call.1 | solution.py:57
  292.6 19.7 %custom-call.29 = f32[4,1,64,64]{2,3,1,0:T(8,128)S(1)} custom-call(f32[4,1,64,64]{3,2,1,0:T(8,128)S(1)} %add_bitcast_fusion.9), custom_call_target="InvertDiagBlocksLowerTriangular" | custom-call | tf_op jit(solution)/shard_map/jvp()/while/body/eval_jaxpr/triangular_solve/custom-call.1 | solution.py:57
  325.5 19.7 %custom-call.29 = f32[4,1,64,64]{2,3,1,0:T(8,128)S(1)} custom-call(f32[4,1,64,64]{3,2,1,0:T(8,128)S(1)} %add_bitcast_fusion.9), custom_call_target="InvertDiagBlocksLowerTriangular" | custom-call | tf_op jit(solution)/shard_map/jvp()/while/body/eval_jaxpr/triangular_solve/custom-call.1 | solution.py:57
  358.4 19.7 %custom-call.29 = f32[4,1,64,64]{2,3,1,0:T(8,128)S(1)} custom-call(f32[4,1,64,64]{3,2,1,0:T(8,128)S(1)} %add_bitcast_fusion.9), custom_call_target="InvertDiagBlocksLowerTriangular" | custom-call | tf_op jit(solution)/shard_map/jvp()/while/body/eval_jaxpr/triangular_solve/custom-call.1 | solution.py:57
  396.2 21.7 %all-reduce.48.cloned.1.call-done = bf16[256,1024]{1,0:T(8,128)(2,1)} async-done(((bf16[256,1024]{1,0:T(8,128)(2,1)}), bf16[256,1024]{1,0:T(8,128)(2,1)}) %all-reduce.48.cloned.1.call-update) | async-done | bytes 524304 | tf_op jit(solution)/shard_map/psum | solution.py:100
  473.0 185.6 %while.116 = (s32[]{:T(128)}, f32[4,128,128]{2,1,0:T(8,128)S(1)}, f32[4,4,64,128]{3,2,0,1:T(8,128)}, f32[4,4,64,128]{3,2,0,1:T(8,128)}, f32[4,4,64,128]{3,2,0,1:...) while((s32[]{:T(128)}, f32[4,128,128]{2,1,0:T(8,128)S(1)}, ...), condition=%wide.region_24.28_spmd.clone, body=%wide.region_21.27_spmd.clone.sunk | while | flops 567340864 | bytes 14615215 | solution.py:70
  475.3 19.7 %custom-call.30 = f32[4,1,64,64]{2,3,1,0:T(8,128)S(1)} custom-call(f32[4,1,64,64]{3,2,1,0:T(8,128)S(1)} %fusion.664), custom_call_target="InvertDiagBlocksLowerTriangular" | custom-call | tf_op jit(solution)/shard_map/transpose(jvp())/while/body/eval_jaxpr/triangular_solve/custom-call.0 | solution.py:57
  521.7 19.7 %custom-call.30 = f32[4,1,64,64]{2,3,1,0:T(8,128)S(1)} custom-call(f32[4,1,64,64]{3,2,1,0:T(8,128)S(1)} %fusion.664), custom_call_target="InvertDiagBlocksLowerTriangular" | custom-call | tf_op jit(solution)/shard_map/transpose(jvp())/while/body/eval_jaxpr/triangular_solve/custom-call.0 | solution.py:57
  568.1 19.7 %custom-call.30 = f32[4,1,64,64]{2,3,1,0:T(8,128)S(1)} custom-call(f32[4,1,64,64]{3,2,1,0:T(8,128)S(1)} %fusion.664), custom_call_target="InvertDiagBlocksLowerTriangular" | custom-call | tf_op jit(solution)/shard_map/transpose(jvp())/while/body/eval_jaxpr/triangular_solve/custom-call.0 | solution.py:57
  614.5 19.7 %custom-call.30 = f32[4,1,64,64]{2,3,1,0:T(8,128)S(1)} custom-call(f32[4,1,64,64]{3,2,1,0:T(8,128)S(1)} %fusion.664), custom_call_target="InvertDiagBlocksLowerTriangular" | custom-call | tf_op jit(solution)/shard_map/transpose(jvp())/while/body/eval_jaxpr/triangular_solve/custom-call.0 | solution.py:57
  758.8 183.0 %while.117 = (s32[]{:T(128)}, f32[4,128,128]{2,1,0:T(8,128)S(1)}, f32[4,4,64,128]{3,2,0,1:T(8,128)}, f32[4,4,64,128]{3,2,0,1:T(8,128)}, f32[4,4,64,128]{3,2,0,1:...) while((s32[]{:T(128)}, f32[4,128,128]{2,1,0:T(8,128)S(1)}, ...), condition=%wide.region_35.39_spmd.clone, body=%wide.region_32.38_spmd.clone.sunk | while | flops 567340864 | bytes 12255863 | solution.py:70
  761.1 19.7 %custom-call.31 = f32[4,1,64,64]{2,3,1,0:T(8,128)S(1)} custom-call(f32[4,1,64,64]{3,2,1,0:T(8,128)S(1)} %fusion.704), custom_call_target="InvertDiagBlocksLowerTriangular" | custom-call | tf_op jit(solution)/shard_map/transpose(jvp())/while/body/eval_jaxpr/triangular_solve/custom-call.0 | solution.py:57
  806.9 19.7 %custom-call.31 = f32[4,1,64,64]{2,3,1,0:T(8,128)S(1)} custom-call(f32[4,1,64,64]{3,2,1,0:T(8,128)S(1)} %fusion.704), custom_call_target="InvertDiagBlocksLowerTriangular" | custom-call | tf_op jit(solution)/shard_map/transpose(jvp())/while/body/eval_jaxpr/triangular_solve/custom-call.0 | solution.py:57
  852.6 19.7 %custom-call.31 = f32[4,1,64,64]{2,3,1,0:T(8,128)S(1)} custom-call(f32[4,1,64,64]{3,2,1,0:T(8,128)S(1)} %fusion.704), custom_call_target="InvertDiagBlocksLowerTriangular" | custom-call | tf_op jit(solution)/shard_map/transpose(jvp())/while/body/eval_jaxpr/triangular_solve/custom-call.0 | solution.py:57
  898.4 19.7 %custom-call.31 = f32[4,1,64,64]{2,3,1,0:T(8,128)S(1)} custom-call(f32[4,1,64,64]{3,2,1,0:T(8,128)S(1)} %fusion.704), custom_call_target="InvertDiagBlocksLowerTriangular" | custom-call | tf_op jit(solution)/shard_map/transpose(jvp())/while/body/eval_jaxpr/triangular_solve/custom-call.0 | solution.py:57
  996.0 437.9 %all-reduce.56.cloned.1.call-done = bf16[12865536]{0:T(1024)(128)(2,1)} async-done(((bf16[12865536]{0:T(1024)(128)(2,1)}), bf16[12865536]{0:T(1024)(128)(2,1)}) %all-reduce.56.cloned.1.call-update) | async-done | bytes 25731088
  1436.1 19.1 reshape.814
  1459.1 17.7 all-reduce.58.cloned.1.call-done
  1478.2 41.0 %all-reduce.33 = (f32[2,128]{1,0:T(2,128)}, f32[2,2,1024]{2,1,0:T(2,128)}) all-reduce(f32[2,128]{1,0:T(2,128)S(1)} %pad_maximum_fusion.11, f32[2,2,1024]{2,1,0:T(2,128)S(1)} %pad_maximum_fusion.10), channel_id=1, replica_groups=mesh['dp'=16,'tensor'=2] {'dp','tensor'}, use_global_device_ids=true, to_apply=%region_51.55 | all-reduce | flops 4352 | bytes 34816 | tf_op jit(solution)/shard_map/psum | solution.py:255
  1522.7 209.9 %all-gather.3.cloned.1.call-done = bf16[16,1,804096]{2,1,0:T(2,128)(2,1)} async-done(((bf16[1,1,804096]{2,1,0:T(2,128)(2,1)}), bf16[16,1,804096]{2,1,0:T(2,128)(2,1)}) %all-gather.3.cloned.1.call-update) | async-done | bytes 25731088 | tf_op jit(solution)/shard_map/all_gather | solution.py:249
  1732.6 58.4 %convert_element_type.283 = f32[16,1,804096]{2,1,0:T(1,128)} convert(bf16[16,1,804096]{2,1,0:T(2,128)(2,1)} %all-gather.3.cloned.1.call-done) | non-fusion elementwise | flops 12865536 | bytes 77193216 | tf_op jit(solution)/shard_map/convert_element_type | solution.py:249
  1812.9 17.0 fusion.453
  1877.0 13.4 stack_reshape.36
  1919.3 16.1 pad_maximum_fusion.4
  (1045 shorter events, 700.7 us)
Async XLA Ops:
  7.2 180.6 %all-reduce.44.cloned.1.call-start = ((), (), s32[]{:S(2)}) async-start(), calls=%async_computation | async-start | bytes 1048576 | tf_op jit(solution)/shard_map/psum | solution.py:100
  9.1 9.9 copy-start.143
  156.3 34.4 %copy-start.93 = (f32[1,1,1024]{2,1,0:T(1,128)S(1)}, f32[1,1,1024]{2,1,0:T(1,128)}, u32[]{:S(2)}) copy-start(f32[1,1,1024]{2,1,0:T(1,128)} %get-tuple-element.2145) | copy-start | bytes 12292
  156.3 71.1 %all-reduce.46.cloned.1.call-start = ((), (), s32[]{:S(2)}) async-start(), calls=%async_computation.1 | async-start | bytes 1048576 | tf_op jit(solution)/shard_map/psum | solution.py:100
  187.8 9.0 slice-start.7
  198.7 219.3 %all-reduce.48.cloned.1.call-start = ((), (), s32[]{:S(2)}) async-start(), calls=%async_computation.2 | async-start | bytes 1048576 | tf_op jit(solution)/shard_map/psum | solution.py:100
  200.9 31.8 %copy-start.83 = (f32[3,1,512]{2,0,1:T(4,128)}, f32[3,1,512]{2,0,1:T(4,128)S(1)}, u32[]{:S(2)}) copy-start(f32[3,1,512]{2,0,1:T(4,128)S(1)} %copy.576) | copy-start | bytes 18436
  200.9 31.8 %copy-start.85 = (f32[3,1,512]{2,0,1:T(4,128)}, f32[3,1,512]{2,0,1:T(4,128)S(1)}, u32[]{:S(2)}) copy-start(f32[3,1,512]{2,0,1:T(4,128)S(1)} %copy.573) | copy-start | bytes 18436
  201.0 31.7 %copy-start.87 = (f32[3,1,512]{2,0,1:T(4,128)}, f32[3,1,512]{2,0,1:T(4,128)S(1)}, u32[]{:S(2)}) copy-start(f32[3,1,512]{2,0,1:T(4,128)S(1)} %copy.574) | copy-start | bytes 18436
  201.0 31.7 %copy-start.89 = (f32[3,1,512]{2,0,1:T(4,128)}, f32[3,1,512]{2,0,1:T(4,128)S(1)}, u32[]{:S(2)}) copy-start(f32[3,1,512]{2,0,1:T(4,128)S(1)} %copy.575) | copy-start | bytes 18436
  201.1 27.7 %copy-start.118 = (f32[256,4]{0,1:T(4,128)}, f32[256,4]{0,1:T(4,128)S(1)}, u32[]{:S(2)}) copy-start(f32[256,4]{0,1:T(4,128)S(1)} %add.446) | copy-start | bytes 12292
  201.1 27.6 %copy-start.91 = (f32[256,4]{0,1:T(4,128)}, f32[256,4]{0,1:T(4,128)S(1)}, u32[]{:S(2)}) copy-start(f32[256,4]{0,1:T(4,128)S(1)} %rsqrt.125) | copy-start | bytes 12292
  202.2 27.1 %copy-start.95 = (f32[1,1,1024]{2,1,0:T(1,128)S(1)}, f32[1,1,1024]{2,1,0:T(1,128)}, u32[]{:S(2)}) copy-start(f32[1,1,1024]{2,1,0:T(1,128)} %get-tuple-element.2128) | copy-start | bytes 12292
  202.7 26.8 %copy-start.102 = (bf16[2,1024,4]{1,2,0:T(4,128)(2,1)S(1)}, bf16[2,1024,4]{1,2,0:T(4,128)(2,1)}, u32[]{:S(2)}) copy-start(bf16[2,1024,4]{1,2,0:T(4,128)(2,1)} %param.27) | copy-start | bytes 49156
  389.2 73.4 %all-reduce.50.cloned.1.call-start = ((), (), s32[]{:S(2)}) async-start(), calls=%async_computation.3 | async-start | bytes 1048576 | tf_op jit(solution)/shard_map/psum | solution.py:104
  396.2 23.0 %copy-start.97 = (f32[1,1,1024]{2,1,0:T(1,128)S(1)}, f32[1,1,1024]{2,1,0:T(1,128)}, u32[]{:S(2)}) copy-start(f32[1,1,1024]{2,1,0:T(1,128)} %get-tuple-element.2127) | copy-start | bytes 12292
  419.2 44.7 %copy-start.135 = (f32[256]{0:T(256)}, f32[256]{0:T(256)S(1)}, u32[]{:S(2)}) copy-start(f32[256]{0:T(256)S(1)} %get-tuple-element.2140) | copy-start | bytes 3076
  419.2 10.4 slice-start.4
  419.2 10.4 slice-start.5
  432.2 271.8 %all-reduce.52.cloned.1.call-start = ((), (), s32[]{:S(2)}) async-start(), calls=%async_computation.4 | async-start | bytes 1048576 | tf_op jit(solution)/shard_map/psum | solution.py:104
  549.5 7.5 copy-start.4
  675.2 73.0 %all-reduce.54.cloned.1.call-start = ((), (), s32[]{:S(2)}) async-start(), calls=%async_computation.5 | async-start | bytes 1048576 | tf_op jit(solution)/shard_map/psum | solution.py:104
  686.7 17.3 copy-start.96
  691.9 13.5 copy-start.141
  691.9 13.5 copy-start.149
  717.7 716.1 %all-reduce.56.cloned.1.call-start = ((), (), s32[]{:S(2)}) async-start(), calls=%async_computation.7 | async-start | bytes 51462144
  961.8 7.8 slice-start.2
  985.1 491.7 %all-reduce.58.cloned.1.call-start = ((), (), s32[]{:S(2)}) async-start(), calls=%async_computation.8 | async-start | bytes 2097152 | tf_op jit(solution)/shard_map/psum | solution.py:100
  994.7 737.9 %all-gather.3.cloned.1.call-start = ((), (), s32[]{:S(2)}) async-start(), calls=%async_computation.6 | async-start | bytes 54678528 | tf_op jit(solution)/shard_map/all_gather | solution.py:249
  1458.6 19.4 copy-start.55
  1476.8 42.4 %copy-start.37 = (bf16[256,1024]{1,0:T(8,128)(2,1)S(1)}, bf16[256,1024]{1,0:T(8,128)(2,1)}, u32[]{:S(2)}) copy-start(bf16[256,1024]{1,0:T(8,128)(2,1)} %get-tuple-element.2032) | copy-start | bytes 1572868
  1877.0 14.6 copy-start.28
  (167 other events, 535.7 us)
Sparse Core Ops, SparseCore 0:
  156.4 31.2 all-reduce.43
  198.8 28.5 all-reduce.45
  389.3 28.5 all-reduce.47
  432.3 28.5 all-reduce.49
  675.4 28.5 all-reduce.51
  717.8 28.5 all-reduce.53
  985.2 448.5 all-reduce.55
  1436.8 39.9 all-reduce.57
  1479.1 253.4 all-gather.2
where the time goes:
time: 1960 us; the launch traced here: 1940 us
  waiting for transfers between devices  756 us (39%)
  other arithmetic  504 us (26%)
  local copies, waits for them, and re-layouts  314 us (16%)
  matrix products  309 us (16%)
  blocking collectives  41 us (2%)
    unnamed x10, waiting for transfers between devices  438 us
    another operation x64, other arithmetic, block_step(): lax.linalg.triangular_solve(unit_lower, right_side, left_side=True, lower...  324 us
    all_gather x1, waiting for transfers between devices, body(): lax.all_gather(shard.astype(jnp.bfloat16), 'dp', axis=0, tiled=True)  210 us
    psum x4, waiting for transfers between devices, branch_total(): lax.psum(partial_value.astype(jnp.bfloat16), 'tensor').astype(jnp.float32)  95.5 us
    unnamed x352, local copies, waits for them, and re-layouts  73.8 us
    convert_element_type x1, other arithmetic, body(): lax.all_gather(shard.astype(jnp.bfloat16), 'dp', axis=0, tiled=True)  58.4 us
    dot_general x24, matrix products, block_step(): jnp.einsum('hid,hjd->hij', query_blk, key_blk, precision=HIGHEST)  45.2 us
    dot_general x24, matrix products, block_step(): result = jnp.einsum('hid,hde->hie', query_blk, memory, precision=HIGHEST)  43 us
  transfers between devices with their start and end apart: 9, of which 7 were waited for; matrix products, arithmetic and copies ran while one was open for 6% of the time, Pallas kernels for 0%

commit v1 on v0

v1 whole, which is shorter than its diff:
```python
import functools
import math

import jax
import jax.numpy as jnp
from jax import lax
from jax.experimental import pallas as pl
from jax.experimental.pallas import tpu as pltpu
from jax.sharding import PartitionSpec as P

DK = 128
KCONV = 4
LAYERS = 2
LANES = 128
F32 = jnp.float32
BF16 = jnp.bfloat16
VMEM_LIMIT = 60 * 1024 * 1024


def dot_nn(a, b):
    return lax.dot_general(a, b, (((1,), (0,)), ((), ())), preferred_element_type=F32)


def dot_nt(a, b):
    return lax.dot_general(a, b, (((1,), (1,)), ((), ())), preferred_element_type=F32)


def dot_tn(a, b):
    return lax.dot_general(a, b, (((0,), (0,)), ((), ())), preferred_element_type=F32)


def halves(a):
    hi = a.astype(BF16)
    return hi, (a - hi.astype(F32)).astype(BF16)


def split_dot(dot, a, b):
    return dot(a[0], b[0]) + (dot(a[0], b[1]) + dot(a[1], b[0]))


def low(a):
    return a.astype(BF16)


def sigmoid(a):
    return 1.0 / (1.0 + jnp.exp(-a))


def rms_scale(a):
    return lax.rsqrt(jnp.mean(a * a, axis=-1, keepdims=True) + 1e-05)


def rms_back(hidden, gain, grad_normed):
    scale = rms_scale(hidden)
    weighted = gain * grad_normed
    inner = jnp.mean(hidden * weighted, axis=-1, keepdims=True)
    grad_hidden = scale * weighted - hidden * (scale * scale * scale) * inner
    rows = jnp.sum(grad_normed * hidden * scale, axis=0, keepdims=True)
    return grad_hidden, rows


def shift_down(a, count):
    if count == 0:
        return a
    row = lax.broadcasted_iota(jnp.int32, a.shape, 0)
    return jnp.where(row >= count, pltpu.roll(a, count, 0), 0.0)


def shift_up(a, count):
    if count == 0:
        return a
    length = a.shape[0]
    row = lax.broadcasted_iota(jnp.int32, a.shape, 0)
    return jnp.where(row < length - count, pltpu.roll(a, length - count, 0), 0.0)


def conv_silu(project, taps):
    total = taps[KCONV - 1 : KCONV, :] * project
    for tap in range(KCONV - 1):
        total = total + taps[tap : tap + 1, :] * shift_down(project, KCONV - 1 - tap)
    gate = sigmoid(total)
    return total, gate, total * gate


def positions(length):
    row = lax.broadcasted_iota(jnp.int32, (length, length), 0)
    col = lax.broadcasted_iota(jnp.int32, (length, length), 1)
    return row, col


def unit_lower_inverse(lower_list):
    length = lower_list[0].shape[0]
    row, col = positions(length)
    eye = jnp.where(row == col, 1.0, 0.0)
    diag_list = [jnp.where(row // 4 == col // 4, lower, 0.0) for lower in lower_list]
    parts = [halves(diag) for diag in diag_list]
    squares = [split_dot(dot_nn, part, part) for part in parts]
    firsts = [eye - diag for diag in diag_list]
    inverse = [
        first + split_dot(dot_nn, halves(first), halves(square))
        for first, square in zip(firsts, squares)
    ]
    size = 4
    while size < length:
        fresh = (row // (2 * size) == col // (2 * size)) & (row // size != col // size)
        offs = [halves(jnp.where(fresh, lower, 0.0)) for lower in lower_list]
        held = [halves(inv) for inv in inverse]
        mids = [split_dot(dot_nn, inv, off) for inv, off in zip(held, offs)]
        inverse = [
            inv - split_dot(dot_nn, halves(mid), part)
            for inv, mid, part in zip(inverse, mids, held)
        ]
        size = 2 * size
    return inverse


def head_cols(head):
    return slice(head * DK, (head + 1) * DK)


def mixer_forward_kernel(level, heads, n_add, *refs):
    (x_ref, *adds) = refs[: 1 + n_add]
    (gain_ref, taps_ref, head_gain_ref, wb_ref, wq_hbm, wo_hbm) = refs[1 + n_add : 7 + n_add]
    (x_out, n1_out, p_out, logit_out, t_out, u_out, o_out, on_out, part_out) = refs[
        7 + n_add : 16 + n_add
    ]
    wq, wo, sems = refs[16 + n_add :]
    loads = [
        pltpu.make_async_copy(wq_hbm.at[level], wq, sems.at[0]),
        pltpu.make_async_copy(wo_hbm.at[level], wo, sems.at[1]),
    ]
    for load in loads:
        load.start()
    x = x_ref[...].astype(F32)
    for add in adds:
        x = x + add[...].astype(F32)
    x_out[...] = x
    length = x.shape[0]
    n1 = low(x * rms_scale(x) * gain_ref[level, 0:1, :].astype(F32))
    n1_out[...] = n1
    logits = dot_nn(n1, wb_ref[level])
    logit_out[...] = logits
    beta = sigmoid(logits)
    loads[0].wait()
    acts = []
    for part in range(3):
        p = dot_nn(n1, wq[part])
        p_out[part] = p
        acts.append(conv_silu(p, taps_ref[level, part].astype(F32))[2])
    row, col = positions(length)
    lowers, scores, values = [], [], []
    for head in range(heads):
        cols = head_cols(head)
        c0, c1, c2 = (act[:, cols] for act in acts)
        q = low(c0 * lax.rsqrt(jnp.sum(c0 * c0, axis=-1, keepdims=True) + 0.001))
        k = low(c1 * lax.rsqrt(jnp.sum(c1 * c1, axis=-1, keepdims=True) + 0.001))
        v = low(c2).astype(F32)
        gate = beta[:, head : head + 1]
        lowers.append(jnp.where(row > col, gate * dot_nt(k, k), 0.0))
        scores.append(low(jnp.where(row >= col, dot_nt(q, k), 0.0)))
        values.append(halves(gate * v))
    inverse = unit_lower_inverse(lowers)
    head_gain = head_gain_ref[level : level + 1, :].astype(F32)
    for head in range(heads):
        cols = head_cols(head)
        t_hi, t_lo = halves(inverse[head])
        t_out[0, head] = t_hi
        t_out[1, head] = t_lo
        u = split_dot(dot_nn, (t_hi, t_lo), values[head])
        u_low = low(u)
        u_out[:, cols] = u_low
        o = dot_nn(scores[head], u_low)
        o_out[:, cols] = o
        scale = lax.rsqrt(jnp.mean(o * o, axis=-1, keepdims=True) + 0.01)
        on_out[:, cols] = low(o * scale * head_gain)
    loads[1].wait()
    part_out[...] = low(dot_nn(on_out[...], wo[...]))


def mixer_forward(level, x, adds, norm_gain, taps, head_gain, wb, wq, wo):
    length, width = x.shape
    chans = wq.shape[-1]
    heads = chans // DK
    sds = jax.ShapeDtypeStruct
    vmem = pl.BlockSpec(memory_space=pltpu.VMEM)
    hbm = pl.BlockSpec(memory_space=pl.ANY)
    return pl.pallas_call(
        functools.partial(mixer_forward_kernel, level, heads, len(adds)),
        out_shape=(
            sds((length, width), F32),
            sds((length, width), BF16),
            sds((3, length, chans), F32),
            sds((length, LANES), F32),
            sds((2, heads, length, length), BF16),
            sds((length, chans), BF16),
            sds((length, chans), F32),
            sds((length, chans), BF16),
            sds((length, width), BF16),
        ),
        in_specs=[vmem] * (5 + len(adds)) + [hbm, hbm],
        out_specs=(vmem,) * 9,
        scratch_shapes=[
            pltpu.VMEM((3, width, chans), BF16),
            pltpu.VMEM((chans, width), BF16),
            pltpu.SemaphoreType.DMA((2,)),
        ],
        compiler_params=pltpu.CompilerParams(vmem_limit_bytes=VMEM_LIMIT),
        name="mixer_forward",
    )(x, *adds, norm_gain, taps, head_gain, wb, wq, wo)


def mlp_forward_kernel(level, n_add, *refs):
    (x_ref, *adds) = refs[: 1 + n_add]
    (gain_ref, wgu_hbm, wd_hbm) = refs[1 + n_add : 4 + n_add]
    (h_out, n2_out, gu_out, z_out, part_out) = refs[4 + n_add : 9 + n_add]
    wgu, wd, sems = refs[9 + n_add :]
    loads = [
        pltpu.make_async_copy(wgu_hbm.at[level, 0], wgu.at[0], sems.at[0]),
        pltpu.make_async_copy(wgu_hbm.at[level, 1], wgu.at[1], sems.at[1]),
        pltpu.make_async_copy(wd_hbm.at[level], wd, sems.at[2]),
    ]
    for load in loads:
        load.start()
    h = x_ref[...].astype(F32)
    for add in adds:
        h = h + add[...].astype(F32)
    h_out[...] = h
    n2 = low(h * rms_scale(h) * gain_ref[level, 1:2, :].astype(F32))
    n2_out[...] = n2
    loads[0].wait()
    g = dot_nn(n2, wgu[0])
    gu_out[0] = g
    loads[1].wait()
    u = dot_nn(n2, wgu[1])
    gu_out[1] = u
    z = low(g * sigmoid(g) * u)
    z_out[...] = z
    loads[2].wait()
    part_out[...] = low(dot_nn(z, wd[...]))


def mlp_forward(level, x, adds, norm_gain, wgu, wd):
    length, width = x.shape
    hidden = wgu.shape[-1]
    sds = jax.ShapeDtypeStruct
    vmem = pl.BlockSpec(memory_space=pltpu.VMEM)
    hbm = pl.BlockSpec(memory_space=pl.ANY)
    return pl.pallas_call(
        functools.partial(mlp_forward_kernel, level, len(adds)),
        out_shape=(
            sds((length, width), F32),
            sds((length, width), BF16),
            sds((2, length, hidden), F32),
            sds((length, hidden), BF16),
            sds((length, width), BF16),
        ),
        in_specs=[vmem] * (2 + len(adds)) + [hbm, hbm],
        out_specs=(vmem,) * 5,
        scratch_shapes=[
            pltpu.VMEM((2, width, hidden), BF16),
            pltpu.VMEM((hidden, width), BF16),
            pltpu.SemaphoreType.DMA((3,)),
        ],
        compiler_params=pltpu.CompilerParams(vmem_limit_bytes=VMEM_LIMIT),
        name="mlp_forward",
    )(x, *adds, norm_gain, wgu, wd)


def back_through_norm(level, which, gain_ref, e_ref, hid_ref, adds, rows_out):
    e = e_ref[...].astype(F32)
    if not adds:
        rows_out[...] = jnp.zeros_like(rows_out)
        return e
    total = adds[0][...].astype(F32)
    for add in adds[1:]:
        total = total + add[...].astype(F32)
    gain = gain_ref[level, which : which + 1, :].astype(F32)
    grad_hidden, rows = rms_back(hid_ref[...], gain, total)
    rows_out[...] = rows
    return e + grad_hidden


def mlp_backward_kernel(level, n_add, *refs):
    (e_ref, hid_ref, *adds) = refs[: 2 + n_add]
    (gain_ref, n2_ref, gu_ref, z_ref, wgu_hbm, wd_hbm) = refs[2 + n_add : 8 + n_add]
    (e_out, rows_out, part_out, gd_out, ggu_out) = refs[8 + n_add : 13 + n_add]
    wgu, wd, dgu_ref, sems = refs[13 + n_add :]
    loads = [
        pltpu.make_async_copy(wd_hbm.at[level], wd, sems.at[0]),
        pltpu.make_async_copy(wgu_hbm.at[level], wgu, sems.at[1]),
    ]
    for load in loads:
        load.start()
    e = back_through_norm(level + 1, 0, gain_ref, e_ref, hid_ref, adds, rows_out)
    e_out[...] = e
    ef = low(e)
    loads[0].wait()
    dz = dot_nt(ef, wd[...])
    g, u = gu_ref[0], gu_ref[1]
    s = sigmoid(g)
    dgu_ref[0] = low(dz * u * (s * (1.0 + g * (1.0 - s))))
    dgu_ref[1] = low(dz * (g * s))
    loads[1].wait()
    part_out[...] = low(dot_nt(dgu_ref[0], wgu[0]) + dot_nt(dgu_ref[1], wgu[1]))
    gd_out[...] = low(dot_tn(z_ref[...], ef))
    for half in range(2):
        ggu_out[half] = low(dot_tn(n2_ref[...], dgu_ref[half]))


def mlp_backward(level, e, hid, adds, norm_gain, n2, gu, z, wgu, wd):
    length, width = e.shape
    hidden = wgu.shape[-1]
    sds = jax.ShapeDtypeStruct
    vmem = pl.BlockSpec(memory_space=pltpu.VMEM)
    hbm = pl.BlockSpec(memory_space=pl.ANY)
    return pl.pallas_call(
        functools.partial(mlp_backward_kernel, level, len(adds)),
        out_shape=(
            sds((length, width), F32),
            sds((1, width), F32),
            sds((length, width), BF16),
            sds((hidden, width), BF16),
            sds((2, width, hidden), BF16),
        ),
        in_specs=[vmem] * (6 + len(adds)) + [hbm, hbm],
        out_specs=(vmem,) * 5,
        scratch_shapes=[
            pltpu.VMEM((2, width, hidden), BF16),
            pltpu.VMEM((hidden, width), BF16),
            pltpu.VMEM((2, length, hidden), BF16),
            pltpu.SemaphoreType.DMA((2,)),
        ],
        compiler_params=pltpu.CompilerParams(vmem_limit_bytes=VMEM_LIMIT),
        name="mlp_backward",
    )(e, hid, *adds, norm_gain, n2, gu, z, wgu, wd)


def mixer_backward_kernel(level, heads, n_add, *refs):
    (e_ref, hid_ref, *adds) = refs[: 2 + n_add]
    (gain_ref, taps_ref, head_gain_ref, wb_ref, n1_ref, p_ref, logit_ref, t_ref, u_ref, o_ref) = (
        refs[2 + n_add : 12 + n_add]
    )
    (on_ref, wq_hbm, wo_hbm) = refs[12 + n_add : 15 + n_add]
    (e_out, rows_out, part_out, gq_out, gc_out, gb_out, gh_out, go_out) = refs[
        15 + n_add : 23 + n_add
    ]
    wq, wo, grads, dp_ref, sems = refs[23 + n_add :]
    loads = [
        pltpu.make_async_copy(wo_hbm.at[level], wo, sems.at[0]),
        pltpu.make_async_copy(wq_hbm.at[level], wq, sems.at[1]),
    ]
    for load in loads:
        load.start()
    e = back_through_norm(level, 1, gain_ref, e_ref, hid_ref, adds, rows_out)
    e_out[...] = e
    em = low(e)
    length = e.shape[0]
    loads[0].wait()
    don = dot_nt(em, wo[...])
    go_out[...] = low(dot_tn(on_ref[...], em))
    beta = sigmoid(logit_ref[...])
    row, col = positions(length)
    lane = lax.broadcasted_iota(jnp.int32, (length, LANES), 1)
    head_gain = head_gain_ref[level : level + 1, :].astype(F32)
    convs = [conv_silu(p_ref[part], taps_ref[level, part].astype(F32)) for part in range(3)]
    gain_rows = jnp.zeros((1, DK), F32)
    dlogit = jnp.zeros((length, LANES), F32)
    for head in range(heads):
        cols = head_cols(head)
        c0, c1, c2 = (conv[2][:, cols] for conv in convs)
        rho0 = lax.rsqrt(jnp.sum(c0 * c0, axis=-1, keepdims=True) + 0.001)
        rho1 = lax.rsqrt(jnp.sum(c1 * c1, axis=-1, keepdims=True) + 0.001)
        q, k, v = low(c0 * rho0), low(c1 * rho1), low(c2).astype(F32)
        gate = beta[:, head : head + 1]
        o = o_ref[:, cols]
        scale = lax.rsqrt(jnp.mean(o * o, axis=-1, keepdims=True) + 0.01)
        dn = don[:, cols]
        weighted = dn * head_gain
        inner = jnp.mean(o * weighted, axis=-1, keepdims=True)
        do = low(scale * weighted - o * (scale * scale * scale) * inner)
        gain_rows = gain_rows + jnp.sum(dn * o * scale, axis=0, keepdims=True)
        u = u_ref[:, cols]
        score_t = low(jnp.where(row <= col, dot_nt(k, q), 0.0))
        du = dot_nn(score_t, do)
        ds = low(jnp.where(row >= col, dot_nt(do, u), 0.0))
        ds_t = low(jnp.where(row <= col, dot_nt(u, do), 0.0))
        dq = dot_nn(ds, k)
        dk = dot_nn(ds_t, q)
        r = split_dot(dot_tn, (t_ref[0, head], t_ref[1, head]), halves(du))
        dv = gate * r
        dv_low = low(dv)
        gram = low(jnp.where(row > col, dot_nt(k, k), 0.0))
        w = v - dot_nn(gram, u)
        dbeta = jnp.sum(r * w, axis=-1, keepdims=True)
        dgram = jnp.where(row > col, dot_nt(dv_low, u), 0.0) + jnp.where(
            row < col, dot_nt(u, dv_low), 0.0
        )
        dk = dk - dot_nn(low(dgram), k)
        grads[0, :, cols] = rho0 * dq - c0 * (rho0 * rho0 * rho0) * jnp.sum(
            c0 * dq, axis=-1, keepdims=True
        )
        grads[1, :, cols] = rho1 * dk - c1 * (rho1 * rho1 * rho1) * jnp.sum(
            c1 * dk, axis=-1, keepdims=True
        )
        grads[2, :, cols] = dv
        dlogit = dlogit + jnp.where(lane == head, dbeta * gate * (1.0 - gate), 0.0)
    gh_out[...] = gain_rows
    dlogit_low = low(dlogit)
    n1 = n1_ref[...]
    gb_out[...] = dot_tn(n1, dlogit_low)
    for part in range(3):
        taps = taps_ref[level, part].astype(F32)
        total, gate, _ = convs[part]
        dsum = grads[part] * (gate * (1.0 + total * (1.0 - gate)))
        p = p_ref[part]
        dp = taps[KCONV - 1 : KCONV, :] * dsum
        for tap in range(KCONV):
            back = KCONV - 1 - tap
            gc_out[part, tap : tap + 1, :] = jnp.sum(
                dsum * shift_down(p, back), axis=0, keepdims=True
            )
            if back:
                dp = dp + taps[tap : tap + 1, :] * shift_up(dsum, back)
        dp_ref[part] = low(dp)
    loads[1].wait()
    dn1 = dot_nt(dlogit_low, wb_ref[level])
    for part in range(3):
        dn1 = dn1 + dot_nt(dp_ref[part], wq[part])
    part_out[...] = low(dn1)
    for part in range(3):
        gq_out[part] = low(dot_tn(n1, dp_ref[part]))


def mixer_backward(level, e, hid, adds, norm_gain, taps, head_gain, wb, kept, wq, wo):
    length, width = e.shape
    chans = wq.shape[-1]
    heads = chans // DK
    sds = jax.ShapeDtypeStruct
    vmem = pl.BlockSpec(memory_space=pltpu.VMEM)
    hbm = pl.BlockSpec(memory_space=pl.ANY)
    return pl.pallas_call(
        functools.partial(mixer_backward_kernel, level, heads, len(adds)),
        out_shape=(
            sds((length, width), F32),
            sds((1, width), F32),
            sds((length, width), BF16),
            sds((3, width, chans), BF16),
            sds((3, KCONV, chans), F32),
            sds((width, LANES), F32),
            sds((1, DK), F32),
            sds((chans, width), BF16),
        ),
        in_specs=[vmem] * (13 + len(adds)) + [hbm, hbm],
        out_specs=(vmem,) * 8,
        scratch_shapes=[
            pltpu.VMEM((3, width, chans), BF16),
            pltpu.VMEM((chans, width), BF16),
            pltpu.VMEM((3, length, chans), F32),
            pltpu.VMEM((3, length, chans), BF16),
            pltpu.SemaphoreType.DMA((2,)),
        ],
        compiler_params=pltpu.CompilerParams(vmem_limit_bytes=VMEM_LIMIT),
        name="mixer_backward",
    )(e, hid, *adds, norm_gain, taps, head_gain, wb, *kept, wq, wo)


def branch_parts(part):
    count = lax.axis_size("tensor")
    if count == 1:
        return (part,)
    if count == 2:
        return (part, lax.ppermute(part, "tensor", [(0, 1), (1, 0)]))
    return (lax.psum(part, "tensor"),)


def sum_over_dp(tables):
    shapes = [table.shape for table in tables]
    flat = jnp.concatenate([table.reshape(-1) for table in tables])
    size = flat.shape[0]
    count = lax.axis_size("dp")
    pad = -size % (count * 1024)
    flat = jnp.pad(flat, (0, pad))
    shard = lax.psum_scatter(flat, "dp", scatter_dimension=0, tiled=True)
    joined = lax.all_gather(shard, "dp", axis=0, tiled=True).astype(F32)
    pieces = []
    offset = 0
    for shape in shapes:
        size = math.prod(shape)
        pieces.append(joined[offset : offset + size].reshape(shape))
        offset = offset + size
    return pieces


def body(
    inputs,
    qkv_weight,
    conv_taps,
    beta_weight,
    out_gain,
    out_weight,
    norm_gain,
    gate_up_weight,
    down_weight,
    cotangent,
):
    heads = beta_weight.shape[-1]
    wb = jnp.pad(beta_weight, ((0, 0), (0, 0), (0, LANES - heads)))
    base, adds = inputs, ()
    kept = []
    for level in range(LAYERS):
        x, n1, p, logits, t, u, o, on, part = mixer_forward(
            level, base, adds, norm_gain, conv_taps, out_gain, wb, qkv_weight, out_weight
        )
        h, n2, gu, z, part_two = mlp_forward(
            level, x, branch_parts(part), norm_gain, gate_up_weight, down_weight
        )
        kept.append((x, h, (n1, p, logits, t, u, o, on), (n2, gu, z)))
        base, adds = h, branch_parts(part_two)
    total = base
    for add in adds:
        total = total + add.astype(F32)
    outputs = total.astype(BF16)

    e, hid, adds = cotangent, kept[-1][0], ()
    gain_rows = {}
    small = [None] * LAYERS
    big = [None] * LAYERS
    for level in reversed(range(LAYERS)):
        x, h, mixer_kept, mlp_kept = kept[level]
        e, rows, part, grad_down, grad_gate_up = mlp_backward(
            level, e, hid, adds, norm_gain, *mlp_kept, gate_up_weight, down_weight
        )
        gain_rows[(level + 1, 0)] = rows
        e, rows, part, grad_qkv, grad_conv, grad_beta, head_rows, grad_out = mixer_backward(
            level,
            e,
            h,
            branch_parts(part),
            norm_gain,
            conv_taps,
            out_gain,
            wb,
            mixer_kept,
            qkv_weight,
            out_weight,
        )
        gain_rows[(level, 1)] = rows
        hid, adds = x, branch_parts(part)
        small[level] = (grad_conv, grad_beta[:, :heads], head_rows[0])
        big[level] = (grad_qkv, grad_out, grad_gate_up, grad_down)
    branch = adds[0].astype(F32)
    for add in adds[1:]:
        branch = branch + add.astype(F32)
    grad_hidden, rows = rms_back(hid, norm_gain[0, 0:1].astype(F32), branch)
    gain_rows[(0, 0)] = rows
    input_grad = (e + grad_hidden).astype(BF16)

    norm_rows = jnp.stack(
        [jnp.concatenate([gain_rows[(level, 0)], gain_rows[(level, 1)]]) for level in range(LAYERS)]
    )
    norm_rows = norm_rows / lax.axis_size("tensor")
    grad_norm, grad_out_gain = lax.psum(
        (norm_rows, jnp.stack([group[2] for group in small])), ("dp", "tensor")
    )
    grad_conv, grad_beta = lax.psum(
        (jnp.stack([group[0] for group in small]), jnp.stack([group[1] for group in small])), "dp"
    )
    sums = [sum_over_dp(big[level]) for level in range(LAYERS)]
    grad_qkv, grad_out, grad_gate_up, grad_down = (
        jnp.stack([sums[level][index] for level in range(LAYERS)]) for index in range(4)
    )
    return (
        outputs,
        input_grad,
        grad_qkv,
        grad_conv,
        grad_beta,
        grad_out_gain,
        grad_out,
        grad_norm,
        grad_gate_up,
        grad_down,
    )


def solution(mesh):
    in_specs = (
        P("dp", None),
        P(None, None, None, "tensor"),
        P(None, None, None, "tensor"),
        P(None, None, "tensor"),
        P(),
        P(None, "tensor", None),
        P(),
        P(None, None, None, "tensor"),
        P(None, "tensor", None),
        P("dp", None),
    )
    out_specs = (
        P("dp", None),
        P("dp", None),
        P(None, None, None, "tensor"),
        P(None, None, None, "tensor"),
        P(None, None, "tensor"),
        P(),
        P(None, "tensor", None),
        P(),
        P(None, None, None, "tensor"),
        P(None, "tensor", None),
    )
    return jax.shard_map(body, mesh=mesh, in_specs=in_specs, out_specs=out_specs, check_vma=False)
```

time: 1960 us -> 1090 us (0.56)
  other arithmetic: 504 us -> 107 us
  matrix products: 309 us -> 0 us
  local copies, waits for them, and re-layouts: 314 us -> 149 us
  waiting for transfers between devices: 756 us -> 650 us
  Pallas kernels: 0 us -> 102 us
    another operation x76 -> x9, other arithmetic: 371 us -> 43.5 us  [the longest x4 42.2 us: body(): jnp.stack([sums[level][index] for level in range(LAYERS)])]
    dot_general x182 -> x0, matrix products: 279 us -> none  [the longest x24 45.2 us: block_step(): jnp.einsum('hid,hjd->hij', query_blk, key_blk, precision=HIGHEST)]
    psum x7 -> x1, waiting for transfers between devices: 108 us -> 0.01 us  [body(): lax.psum((jnp.stack([group[0] for group in small]), jnp.stack([group[1] f...]
    pallas_call x0 -> x8, Pallas kernels: none -> 102 us  [the longest x2 30.3 us: mixer_forward(): pl.pallas_call(functools.partial(mixer_forward_kernel, level, heads, len(...]
    all_gather x1 -> x2, waiting for transfers between devices: 210 us -> 126 us  [sum_over_dp(): joined = lax.all_gather(shard, 'dp', axis=0, tiled=True).astype(F32)]
    ppermute x0 -> x8, waiting for transfers between devices: none -> 75.9 us  [branch_parts(): return (part, lax.ppermute(part, 'tensor', [(0, 1), (1, 0)]))]
    convert_element_type x20 -> x3, other arithmetic: 69.3 us -> 4.61 us  [the longest x1 2.37 us: body(): input_grad = (e + grad_hidden).astype(BF16)]
    concatenate x0 -> x1, other arithmetic: none -> 58.6 us  [sum_over_dp(): flat = jnp.concatenate([table.reshape(-1) for table in tables])]
  transfers between devices with their start and end apart: 9 -> 12, of which waited for: 7 -> 10; matrix products, arithmetic and copies ran while one was open for 6% -> 17% of each run, Pallas kernels for 0% -> 0%
where the time goes in v1:
time: 1090 us; the launch traced here: 1080 us
  waiting for transfers between devices  650 us (60%)
  local copies, waits for them, and re-layouts  149 us (14%)
  other arithmetic  107 us (10%)
  Pallas kernels  102 us (9%)
  blocking collectives  43.3 us (4%)
  between operations  15.2 us (1%)
  starting transfers between devices  12.1 us (1%)
    unnamed x5, waiting for transfers between devices  448 us
    all_gather x2, waiting for transfers between devices, sum_over_dp(): joined = lax.all_gather(shard, 'dp', axis=0, tiled=True).astype(F32)  126 us
    ppermute x8, waiting for transfers between devices, branch_parts(): return (part, lax.ppermute(part, 'tensor', [(0, 1), (1, 0)]))  75.9 us
    concatenate x1, other arithmetic, sum_over_dp(): flat = jnp.concatenate([table.reshape(-1) for table in tables])  58.6 us
    another operation x8, local copies, waits for them, and re-layouts, body(): jnp.stack([sums[level][index] for level in range(LAYERS)])  57.7 us
    psum x1, blocking collectives, body(): lax.psum((norm_rows, jnp.stack([group[2] for group in small])), ('dp', 't...  43.3 us
    another operation x4, other arithmetic, body(): jnp.stack([sums[level][index] for level in range(LAYERS)])  42.2 us
    slice x8, local copies, waits for them, and re-layouts, sum_over_dp(): pieces.append(joined[offset:offset + size].reshape(shape))  33.5 us
  transfers between devices with their start and end apart: 12, of which 10 were waited for; matrix products, arithmetic and copies ran while one was open for 17% of the time, Pallas kernels for 0%

profile of v1, /device:TPU:0, one launch (start us, length us, event | category | flops | bytes accessed | tf_op | source)
XLA Modules:
  0.0 1078.1 jit_solution(1304030503302155499)
XLA Ops:
  9.2 14.9 %mixer_forward.2 = (f32[256,1024]{1,0:T(8,128)}, bf16[256,1024]{1,0:T(8,128)(2,1)}, f32[3,256,512]{2,1,0:T(8,128)}, f32[256,128]{1,0:T(8,128)}, bf16[2,4,256,256...) custom-call(bf16[256,1024]{1,0:T(8,128)(2,1)} %refs_0_.2, ...), custom_call_target="tpu_custom_call" | custom-call | tf_op jit(solution)/shard_map/mixer_forward/pallas_call | solution.py:187
  27.1 12.1 %collective-permute-done.refs_2_ = bf16[256,1024]{1,0:T(8,128)(2,1)S(1)} collective-permute-done((bf16[256,1024]{1,0:T(8,128)(2,1)}, bf16[256,1024]{1,0:T(8,128)(2,1)S(1)}, u32[]{:S(2)}, u32[]{:S(2)}) %collective-permute-start) | collective-permute-done | bytes 524320 | tf_op jit(solution)/shard_map/ppermute | solution.py:472
  40.0 7.9 mlp_forward.2
  49.7 11.6 %collective-permute-done.1.refs_2_ = bf16[256,1024]{1,0:T(8,128)(2,1)S(1)} collective-permute-done((bf16[256,1024]{1,0:T(8,128)(2,1)}, bf16[256,1024]{1,0:T(8,128)(2,1)S(1)}, u32[]{:S(2)}, u32[]{:S(2)}) %collective-permute-start.1) | collective-permute-done | bytes 524320 | tf_op jit(solution)/shard_map/ppermute | solution.py:472
  62.0 15.4 %mixer_forward.3 = (f32[256,1024]{1,0:T(8,128)}, bf16[256,1024]{1,0:T(8,128)(2,1)}, f32[3,256,512]{2,1,0:T(8,128)}, f32[256,128]{1,0:T(8,128)}, bf16[2,4,256,256...) custom-call(f32[256,1024]{1,0:T(8,128)} %get-tuple-element.65.refs_0, ...), custom_call_target="tpu_custom_call" | custom-call | tf_op jit(solution)/shard_map/mixer_forward/pallas_call | solution.py:187
  78.9 11.0 %collective-permute-done.2.refs_2_ = bf16[256,1024]{1,0:T(8,128)(2,1)S(1)} collective-permute-done((bf16[256,1024]{1,0:T(8,128)(2,1)}, bf16[256,1024]{1,0:T(8,128)(2,1)S(1)}, u32[]{:S(2)}, u32[]{:S(2)}) %collective-permute-start.2) | collective-permute-done | bytes 524320 | tf_op jit(solution)/shard_map/ppermute | solution.py:472
  90.7 8.1 mlp_forward.3
  98.8 12.9 %mlp_backward.2 = (f32[256,1024]{1,0:T(8,128)}, f32[1,1024]{1,0:T(1,128)}, bf16[256,1024]{1,0:T(8,128)(2,1)}, bf16[1408,1024]{1,0:T(8,128)(2,1)}, bf16[2,1024,1408]{2,1,0:T(8,128)(2,1)}) custom-call(bf16[256,1024]{1,0:T(8,128)(2,1)} %refs_0_.3, f32[256,1024]{1,0:T(8,128)} %get-tuple-element.67.refs_0_.refs_1_, bf16[2,2,1024]{2,1,0:T(2,128)(2,1)} %refs_4_.11, ...), custom_call_target="tpu_custom_call" | custom-call | tf_op jit(solution)/shard_map/mlp_backward/pallas_call | solution.py:316
  112.8 10.4 collective-permute-done.4.refs_3_
  124.0 14.7 %mixer_backward.2 = (f32[256,1024]{1,0:T(8,128)}, f32[1,1024]{1,0:T(1,128)}, bf16[256,1024]{1,0:T(8,128)(2,1)}, bf16[3,1024,512]{2,1,0:T(8,128)(2,1)}, f32[3,4,5...) custom-call(f32[256,1024]{1,0:T(8,128)} %get-tuple-element.74.refs_0_, ...), custom_call_target="tpu_custom_call" | custom-call | tf_op jit(solution)/shard_map/mixer_backward/pallas_call | solution.py:441
  139.5 9.8 collective-permute-done.5.refs_3_
  150.1 13.5 %mlp_backward.3 = (f32[256,1024]{1,0:T(8,128)}, f32[1,1024]{1,0:T(1,128)}, bf16[256,1024]{1,0:T(8,128)(2,1)}, bf16[1408,1024]{1,0:T(8,128)(2,1)}, bf16[2,1024,1408]{2,1,0:T(8,128)(2,1)}) custom-call(f32[256,1024]{1,0:T(8,128)} %get-tuple-element.83.refs_0_, f32[256,1024]{1,0:T(8,128)} %get-tuple-element.67.refs_0_.refs_1_, ...), custom_call_target="tpu_custom_call" | custom-call | tf_op jit(solution)/shard_map/mlp_backward/pallas_call | solution.py:316
  166.5 11.8 %reshape.77 = bf16[2883584]{0:T(1024)(128)(2,1)} reshape(bf16[2,1024,1408]{2,1,0:T(8,128)(2,1)} %get-tuple-element.105) | data formatting | bytes 11534336 | tf_op jit(solution)/shard_map/reshape | solution.py:478
  188.5 12.0 %reshape.73 = bf16[2883584]{0:T(1024)(128)(2,1)} reshape(bf16[2,1024,1408]{2,1,0:T(8,128)(2,1)} %get-tuple-element.101) | data formatting | bytes 11534336 | tf_op jit(solution)/shard_map/reshape | solution.py:478
  200.4 14.3 %mixer_backward.3 = (f32[256,1024]{1,0:T(8,128)}, f32[1,1024]{1,0:T(1,128)}, bf16[256,1024]{1,0:T(8,128)(2,1)}, bf16[3,1024,512]{2,1,0:T(8,128)(2,1)}, f32[3,4,5...) custom-call(f32[256,1024]{1,0:T(8,128)} %get-tuple-element.88.refs_0_, ...), custom_call_target="tpu_custom_call" | custom-call | tf_op jit(solution)/shard_map/mixer_backward/pallas_call | solution.py:441
  219.8 58.6 %pad_maximum_fusion.1 = (bf16[6422528]{0:T(1024)(128)(2,1)}, bf16[6422528]{0:T(1024)(128)(2,1)}) fusion(bf16[1441792]{0:T(1024)(128)(2,1)} %bitcast.30, bf16[2883584]{0:T(1024)(128)(2,1)} %reshape.73, bf16[524288]{0:T(1024)(128)(2,1)S(1)} %bitcast.32, bf16[1572864]{0:T(1024)(128)(2,1)S(1)} %bitcast.28, bf16[1441792]{0:T(1024)(128)(2,1)} %bitcast.29, ...), kind=kLoop, calls=%fused_computation.1 | loop fusion | flops 102760448 | bytes 51380224 | tf_op jit(solution)/shard_map/concatenate | solution.py:478
  280.3 448.1 %all-reduce.11.cloned.1.call-done = (bf16[6422528]{0:T(1024)(128)(2,1)}, bf16[6422528]{0:T(1024)(128)(2,1)}) async-done(((bf16[6422528]{0:T(1024)(128)(2,1)}, bf16[6422528]{0:T(1024)(128)(2,1)}), (bf16[6422528]{0:T(1024)(128)(2,1)}, bf16[6422528]{0:T(1024)(128)(2,1)})) %all-reduce.11.cloned.1.call-update) | async-done | bytes 25690128
  735.6 11.7 %collective-permute-done.3 = bf16[256,1024]{1,0:T(8,128)(2,1)} collective-permute-done((bf16[256,1024]{1,0:T(8,128)(2,1)}, bf16[256,1024]{1,0:T(8,128)(2,1)}, u32[]{:S(2)}, u32[]{:S(2)}) %collective-permute-start.3) | collective-permute-done | bytes 524320 | tf_op jit(solution)/shard_map/ppermute | solution.py:472
  753.8 9.3 collective-permute-done.7
  763.6 43.3 %all-reduce.3 = (f32[2,128]{1,0:T(2,128)}, f32[2,2,1024]{2,1,0:T(2,128)}) all-reduce(f32[2,128]{1,0:T(2,128)S(1)} %pad_maximum_fusion.8, f32[2,2,1024]{2,1,0:T(2,128)S(1)} %maximum_multiply_fusion), channel_id=1, replica_groups=mesh['dp'=16,'tensor'=2] {'dp','tensor'}, use_global_device_ids=true, to_apply=%region_6.7 | all-reduce | flops 4352 | bytes 34816 | tf_op jit(solution)/shard_map/psum | solution.py:562
  809.3 24.9 %all-gather.3.cloned.1.call-done = bf16[6422528]{0:T(1024)(128)(2,1)} async-done(((bf16[401408]{0:T(1024)(128)(2,1)}), bf16[6422528]{0:T(1024)(128)(2,1)}) %all-gather.3.cloned.1.call-update) | async-done | bytes 12845072 | tf_op jit(solution)/shard_map/all_gather | solution.py:484
  837.1 100.6 %all-gather.5.cloned.1.call-done = bf16[6422528]{0:T(1024)(128)(2,1)} async-done(((bf16[401408]{0:T(1024)(128)(2,1)}), bf16[6422528]{0:T(1024)(128)(2,1)}) %all-gather.5.cloned.1.call-update) | async-done | bytes 12845072 | tf_op jit(solution)/shard_map/all_gather | solution.py:484
  944.6 6.9 stack_reshape.30
  962.6 7.0 slice.48
  969.6 13.3 %stack_reshape.28 = f32[1,2,1024,1408]{3,2,1,0:T(8,128)} reshape(f32[2883584]{0:T(1024)} %slice.48) | data formatting | bytes 23068672 | tf_op jit(solution)/shard_map/stack;reshape | solution.py:570
  987.2 7.2 stack_reshape.24
  994.4 7.0 slice.49
  1001.4 13.2 %stack_reshape.29 = f32[1,2,1024,1408]{3,2,1,0:T(8,128)} reshape(f32[2883584]{0:T(1024)} %slice.49) | data formatting | bytes 23068672 | tf_op jit(solution)/shard_map/stack;reshape | solution.py:570
  1018.9 7.2 stack_reshape.25
  1026.1 11.4 %pad_maximum_fusion.4 = f32[2,1408,1024]{2,1,0:T(8,128)} fusion(f32[1,1408,1024]{2,1,0:T(8,128)} %stack_reshape.31, f32[1,1408,1024]{2,1,0:T(8,128)} %stack_reshape.30), kind=kLoop, calls=%fused_computation.4 | loop fusion | flops 2883584 | bytes 23068672 | tf_op jit(solution)/shard_map/stack | solution.py:570
  1037.5 16.3 %pad_maximum_fusion = f32[2,2,1024,1408]{3,2,1,0:T(8,128)} fusion(f32[1,2,1024,1408]{3,2,1,0:T(8,128)} %stack_reshape.29, f32[1,2,1024,1408]{3,2,1,0:T(8,128)} %stack_reshape.28), kind=kLoop, calls=%fused_computation | loop fusion | flops 5767168 | bytes 46137344 | tf_op jit(solution)/shard_map/stack | solution.py:570
  1053.8 9.7 pad_maximum_fusion.3
  (99 shorter events, 87.0 us)
Async XLA Ops:
  7.2 721.2 %all-reduce.11.cloned.1.call-start = ((), (), s32[]{:S(2)}) async-start(), calls=%async_computation.3 | async-start | bytes 51380224
  24.1 15.1 %collective-permute-start = (bf16[256,1024]{1,0:T(8,128)(2,1)}, bf16[256,1024]{1,0:T(8,128)(2,1)S(1)}, u32[]{:S(2)}, u32[]{:S(2)}) collective-permute-start(bf16[256,1024]{1,0:T(8,128)(2,1)} %get-tuple-element.64.refs_1_), channel_id=1, source_target_pairs={{0,1},{1,0},{2,3},{3,2},{4,5},{5,4},{6,7},{7,6},{8,9},{9,8},{10,11... | collective-permute-start | bytes 1572872 | tf_op jit(solution)/shard_map/ppermute | solution.py:472
  39.2 0.8 copy-start.8
  47.9 13.4 %collective-permute-start.1 = (bf16[256,1024]{1,0:T(8,128)(2,1)}, bf16[256,1024]{1,0:T(8,128)(2,1)S(1)}, u32[]{:S(2)}, u32[]{:S(2)}) collective-permute-start(bf16[256,1024]{1,0:T(8,128)(2,1)} %get-tuple-element.66.refs_1_), channel_id=1, source_target_pairs={{0,1},{1,0},{2,3},{3,2},{4,5},{5,4},{6,7},{7,6},{8,9},{9,8},{10,11... | collective-permute-start | bytes 1572872 | tf_op jit(solution)/shard_map/ppermute | solution.py:472
  61.3 0.8 copy-start.7
  77.4 12.5 %collective-permute-start.2 = (bf16[256,1024]{1,0:T(8,128)(2,1)}, bf16[256,1024]{1,0:T(8,128)(2,1)S(1)}, u32[]{:S(2)}, u32[]{:S(2)}) collective-permute-start(bf16[256,1024]{1,0:T(8,128)(2,1)} %get-tuple-element.68.refs_1_), channel_id=1, source_target_pairs={{0,1},{1,0},{2,3},{3,2},{4,5},{5,4},{6,7},{7,6},{8,9},{9,8},{10,11... | collective-permute-start | bytes 1572872 | tf_op jit(solution)/shard_map/ppermute | solution.py:472
  89.9 0.8 copy-start.9
  111.7 11.5 %collective-permute-start.4 = (bf16[256,1024]{1,0:T(8,128)(2,1)}, bf16[256,1024]{1,0:T(8,128)(2,1)S(1)}, u32[]{:S(2)}, u32[]{:S(2)}) collective-permute-start(bf16[256,1024]{1,0:T(8,128)(2,1)} %get-tuple-element.75.refs_2_), channel_id=1, source_target_pairs={{0,1},{1,0},{2,3},{3,2},{4,5},{5,4},{6,7},{7,6},{8,9},{9,8},{10,11... | collective-permute-start | bytes 1572872 | tf_op jit(solution)/shard_map/ppermute | solution.py:472
  123.2 0.8 copy-start.5
  138.7 10.6 collective-permute-start.5
  149.3 0.8 copy-start.6
  150.1 14.0 %copy-start.2 = (bf16[1408,1024]{1,0:T(8,128)(2,1)S(1)}, bf16[1408,1024]{1,0:T(8,128)(2,1)}, u32[]{:S(2)}) copy-start(bf16[1408,1024]{1,0:T(8,128)(2,1)} %get-tuple-element.106) | copy-start | bytes 8650756
  163.6 36.9 %collective-permute-start.6 = (bf16[256,1024]{1,0:T(8,128)(2,1)}, bf16[256,1024]{1,0:T(8,128)(2,1)}, u32[]{:S(2)}, u32[]{:S(2)}) collective-permute-start(bf16[256,1024]{1,0:T(8,128)(2,1)} %get-tuple-element.89.refs_2_), channel_id=1, source_target_pairs={{0,1},{1,0},{2,3},{3,2},{4,5},{5,4},{6,7},{7,6},{8,9},{9,8},{10,11... | collective-permute-start | bytes 1572872 | tf_op jit(solution)/shard_map/ppermute | solution.py:472
  278.4 0.7 copy-start.17
  278.4 454.3 %copy-start = (f32[256,1024]{1,0:T(8,128)S(1)}, f32[256,1024]{1,0:T(8,128)}, u32[]{:S(2)}) copy-start(f32[256,1024]{1,0:T(8,128)} %get-tuple-element.63.refs_0_) | copy-start | bytes 3145732
  278.4 456.0 %copy-start.4 = (bf16[2,2,1024]{2,1,0:T(2,128)(2,1)S(1)}, bf16[2,2,1024]{2,1,0:T(2,128)(2,1)}, u32[]{:S(2)}) copy-start(bf16[2,2,1024]{2,1,0:T(2,128)(2,1)} %refs_4_.11) | copy-start | bytes 24580
  278.4 469.0 %copy-start.1 = (f32[256,1024]{1,0:T(8,128)S(1)}, f32[256,1024]{1,0:T(8,128)}, u32[]{:S(2)}) copy-start(f32[256,1024]{1,0:T(8,128)} %get-tuple-element.69.refs_1_) | copy-start | bytes 3145732
  278.4 471.2 %copy-start.12 = (f32[1,1024]{1,0:T(1,128)S(1)}, f32[1,1024]{1,0:T(1,128)}, u32[]{:S(2)}) copy-start(f32[1,1024]{1,0:T(1,128)} %get-tuple-element.115) | copy-start | bytes 12292
  278.4 471.2 %copy-start.14 = (f32[1,1024]{1,0:T(1,128)S(1)}, f32[1,1024]{1,0:T(1,128)}, u32[]{:S(2)}) copy-start(f32[1,1024]{1,0:T(1,128)} %get-tuple-element.114) | copy-start | bytes 12292
  278.4 471.2 %copy-start.3 = (bf16[256,1024]{1,0:T(8,128)(2,1)S(1)}, bf16[256,1024]{1,0:T(8,128)(2,1)}, u32[]{:S(2)}) copy-start(bf16[256,1024]{1,0:T(8,128)(2,1)} %get-tuple-element.98) | copy-start | bytes 1572868
  278.5 474.6 %copy-start.10 = (f32[3,4,512]{2,1,0:T(4,128)S(1)}, f32[3,4,512]{2,1,0:T(4,128)}, u32[]{:S(2)}) copy-start(f32[3,4,512]{2,1,0:T(4,128)} %get-tuple-element.108) | copy-start | bytes 73732
  278.5 474.6 %copy-start.11 = (f32[3,4,512]{2,1,0:T(4,128)S(1)}, f32[3,4,512]{2,1,0:T(4,128)}, u32[]{:S(2)}) copy-start(f32[3,4,512]{2,1,0:T(4,128)} %get-tuple-element.107) | copy-start | bytes 73732
  278.5 475.3 %copy-start.15 = (f32[1,128]{1,0:T(1,128)S(1)}, f32[1,128]{1,0:T(1,128)}, u32[]{:S(2)}) copy-start(f32[1,128]{1,0:T(1,128)} %get-tuple-element.112) | copy-start | bytes 1540
  278.5 475.3 %copy-start.16 = (f32[1,128]{1,0:T(1,128)S(1)}, f32[1,128]{1,0:T(1,128)}, u32[]{:S(2)}) copy-start(f32[1,128]{1,0:T(1,128)} %get-tuple-element.111) | copy-start | bytes 1540
  278.5 485.1 %copy-start.13 = (f32[1,1024]{1,0:T(1,128)S(1)}, f32[1,1024]{1,0:T(1,128)}, u32[]{:S(2)}) copy-start(f32[1,1024]{1,0:T(1,128)} %get-tuple-element.113) | copy-start | bytes 12292
  278.5 555.8 %all-gather.3.cloned.1.call-start = ((), (), s32[]{:S(2)}) async-start(), calls=%async_computation | async-start | bytes 13647872 | tf_op jit(solution)/shard_map/all_gather | solution.py:484
  730.4 207.3 %all-gather.5.cloned.1.call-start = ((), (), s32[]{:S(2)}) async-start(), calls=%async_computation.1 | async-start | bytes 13647872 | tf_op jit(solution)/shard_map/all_gather | solution.py:484
  732.6 335.7 %all-reduce.9.cloned.1.call-start = ((), (), s32[]{:S(2)}) async-start(), calls=%async_computation.2 | async-start | bytes 163840 | tf_op jit(solution)/shard_map/psum | solution.py:565
  732.8 14.6 %collective-permute-start.3 = (bf16[256,1024]{1,0:T(8,128)(2,1)}, bf16[256,1024]{1,0:T(8,128)(2,1)}, u32[]{:S(2)}, u32[]{:S(2)}) collective-permute-start(bf16[256,1024]{1,0:T(8,128)(2,1)} %get-tuple-element.70), channel_id=1, source_target_pairs={{0,1},{1,0},{2,3},{3,2},{4,5},{5,4},{6,7},{7,6},{8,9},{9,8},{10,11... | collective-permute-start | bytes 1572872 | tf_op jit(solution)/shard_map/ppermute | solution.py:472
  749.6 13.4 %collective-permute-start.7 = (bf16[256,1024]{1,0:T(8,128)(2,1)S(1)}, bf16[256,1024]{1,0:T(8,128)(2,1)S(1)}, u32[]{:S(2)}, u32[]{:S(2)}) collective-permute-start(bf16[256,1024]{1,0:T(8,128)(2,1)S(1)} %copy-done.3), channel_id=1, source_target_pairs={{0,1},{1,0},{2,3},{3,2},{4,5},{5,4},{6,7},{7,6},{8,9},{9,8},{10,11... | collective-permute-start | bytes 1572872 | tf_op jit(solution)/shard_map/ppermute | solution.py:472
  1026.1 27.7 %slice-start = ((s8[6291456]{0:T(1024)(128)(4,1)}), s8[4194304]{0:T(1024)(128)(4,1)S(1)}, s32[]{:S(2)}) async-start(s8[6291456]{0:T(1024)(128)(4,1)} %bitcast.25), calls=%async_computation.4 | async-start | bytes 8388608
  1037.5 16.3 %slice-start.1 = ((s8[6291456]{0:T(1024)(128)(4,1)}), s8[2097152]{0:T(1024)(128)(4,1)S(1)}, s32[]{:S(2)}) async-start(s8[6291456]{0:T(1024)(128)(4,1)} %bitcast.25), calls=%async_computation.5 | async-start | bytes 4194304
Sparse Core Ops, SparseCore 0:
  278.6 449.7 all-reduce.10
  731.2 103.0 all-gather.2
  837.1 100.5 all-gather.4
  941.7 83.7 all-reduce.8

commit v2 on v1

--- a/solution.py
+++ b/solution.py
@@ -12,6 +12,7 @@
 KCONV = 4
 LAYERS = 2
 LANES = 128
+SIDE = 512
 F32 = jnp.float32
 BF16 = jnp.bfloat16
 VMEM_LIMIT = 60 * 1024 * 1024
@@ -341,10 +342,8 @@
         refs[2 + n_add : 12 + n_add]
     )
     (on_ref, wq_hbm, wo_hbm) = refs[12 + n_add : 15 + n_add]
-    (e_out, rows_out, part_out, gq_out, gc_out, gb_out, gh_out, go_out) = refs[
-        15 + n_add : 23 + n_add
-    ]
-    wq, wo, grads, dp_ref, sems = refs[23 + n_add :]
+    (e_out, part_out, small_out, gq_out, go_out) = refs[15 + n_add : 20 + n_add]
+    wq, wo, grads, dp_ref, rows_out, sems = refs[20 + n_add :]
     loads = [
         pltpu.make_async_copy(wo_hbm.at[level], wo, sems.at[0]),
         pltpu.make_async_copy(wq_hbm.at[level], wq, sems.at[1]),
@@ -404,10 +403,15 @@
         )
         grads[2, :, cols] = dv
         dlogit = dlogit + jnp.where(lane == head, dbeta * gate * (1.0 - gate), 0.0)
-    gh_out[...] = gain_rows
+    chans = grads.shape[-1]
+    small_out[...] = jnp.zeros_like(small_out)
+    small_out[0:1, SIDE : SIDE + DK] = gain_rows
+    half = rows_out.shape[-1] // 2
+    small_out[1:2, SIDE:] = rows_out[:, :half]
+    small_out[2:3, SIDE:] = rows_out[:, half:]
     dlogit_low = low(dlogit)
     n1 = n1_ref[...]
-    gb_out[...] = dot_tn(n1, dlogit_low)
+    small_out[3 * KCONV : 3 * KCONV + heads, :] = dot_tn(dlogit_low, n1)[:heads, :]
     for part in range(3):
         taps = taps_ref[level, part].astype(F32)
         total, gate, _ = convs[part]
@@ -416,7 +420,8 @@
         dp = taps[KCONV - 1 : KCONV, :] * dsum
         for tap in range(KCONV):
             back = KCONV - 1 - tap
-            gc_out[part, tap : tap + 1, :] = jnp.sum(
+            spot = part * KCONV + tap
+            small_out[spot : spot + 1, :chans] = jnp.sum(
                 dsum * shift_down(p, back), axis=0, keepdims=True
             )
             if back:
@@ -442,21 +447,19 @@
         functools.partial(mixer_backward_kernel, level, heads, len(adds)),
         out_shape=(
             sds((length, width), F32),
-            sds((1, width), F32),
             sds((length, width), BF16),
+            sds((16, width), F32),
             sds((3, width, chans), BF16),
-            sds((3, KCONV, chans), F32),
-            sds((width, LANES), F32),
-            sds((1, DK), F32),
             sds((chans, width), BF16),
         ),
         in_specs=[vmem] * (13 + len(adds)) + [hbm, hbm],
-        out_specs=(vmem,) * 8,
+        out_specs=(vmem,) * 5,
         scratch_shapes=[
             pltpu.VMEM((3, width, chans), BF16),
             pltpu.VMEM((chans, width), BF16),
             pltpu.VMEM((3, length, chans), F32),
             pltpu.VMEM((3, length, chans), BF16),
+            pltpu.VMEM((1, width), F32),
             pltpu.SemaphoreType.DMA((2,)),
         ],
         compiler_params=pltpu.CompilerParams(vmem_limit_bytes=VMEM_LIMIT),
@@ -481,7 +484,7 @@
     pad = -size % (count * 1024)
     flat = jnp.pad(flat, (0, pad))
     shard = lax.psum_scatter(flat, "dp", scatter_dimension=0, tiled=True)
-    joined = lax.all_gather(shard, "dp", axis=0, tiled=True).astype(F32)
+    joined = lax.all_gather(shard, "dp", axis=0, tiled=True)
     pieces = []
     offset = 0
     for shape in shapes:
@@ -489,6 +492,269 @@
         pieces.append(joined[offset : offset + size].reshape(shape))
         offset = offset + size
     return pieces
+
+
+def ring_place(n_dp):
+    spot = lax.axis_index("dp")
+    core = lax.rem(spot, 2)
+    side = lax.rem(lax.div(spot, 2), 2)
+    depth = lax.div(spot, 4)
+    length = n_dp // 2
+    return core, depth + side * (length - 1 - 2 * depth), length
+
+
+def ring_spot(place, core, length):
+    side = lax.div(place, length // 2)
+    depth = place + side * (length - 1 - 2 * place)
+    return (depth * 2 + side) * 2 + core
+
+
+def ring_kernel(n_dp, kinds, *refs):
+    count = len(kinds)
+    given = refs[:count]
+    total = refs[count : 2 * count]
+    own = refs[2 * count : 3 * count]
+    peer = refs[3 * count : 4 * count]
+    slots = refs[4 * count : 5 * count]
+    load_sem, core_sems, send_sems, recv_sems, fan_sems, keep_sem = refs[5 * count :]
+    core, place, length = ring_place(n_dp)
+    partner = {"dp": ring_spot(place, 1 - core, length)}
+    places = [lax.rem(place + 1, length), lax.rem(place + length - 1, length)]
+    nexts = [{"dp": ring_spot(spot, core, length)} for spot in places]
+    streams = [(index, way) for index in range(count) for way in range(2)]
+
+    def share(ref, index, half):
+        kind = kinds[index]
+        if kind == "rows":
+            return ref.at[:, half]
+        if kind == "cols":
+            wide = ref.shape[-1] // 2
+            return ref.at[:, :, pl.ds(pl.multiple_of(half * wide, LANES), wide)]
+        return ref.at[half]
+
+    def piece(ref, index, chunk, way):
+        kind = kinds[index]
+        if kind == "rows":
+            high = ref.shape[1] // 2
+            return ref.at[chunk, way * high : (way + 1) * high]
+        if kind == "cols":
+            wide = ref.shape[-1] // 2
+            return ref.at[chunk, :, way * wide : (way + 1) * wide]
+        return ref.at[way, :, pl.ds(pl.multiple_of(chunk * LANES, LANES), LANES)]
+
+    def spot_of(ref, index, half, chunk, way):
+        kind = kinds[index]
+        if kind == "rows":
+            high = ref.shape[2] // 2
+            return ref.at[chunk, half, way * high : (way + 1) * high]
+        if kind == "cols":
+            wide = ref.shape[-1] // 4
+            start = pl.multiple_of(half * (2 * wide) + way * wide, LANES)
+            return ref.at[chunk, :, pl.ds(start, wide)]
+        return ref.at[half, way, :, pl.ds(pl.multiple_of(chunk * LANES, LANES), LANES)]
+
+    def turned(way, steps):
+        if way == 0:
+            return lax.rem(place + 2 * length - steps, length)
+        return lax.rem(place + steps + length, length)
+
+    def remote(source, target, send, recv, device):
+        return pltpu.make_async_remote_copy(
+            src_ref=source,
+            dst_ref=target,
+            send_sem=send,
+            recv_sem=recv,
+            device_id=device,
+            device_id_type=pl.DeviceIdType.MESH,
+        )
+
+    def scatter_copy(index, way, step):
+        return remote(
+            piece(own[index], index, turned(way, step), way),
+            slots[index].at[way, step],
+            send_sems.at[0, index, way, step],
+            recv_sems.at[0, index, way, step],
+            nexts[way],
+        )
+
+    def gather_copy(index, way, step, first):
+        chunk = turned(way, step - 1 + length)
+        target = spot_of(total[index], index, core, chunk, way)
+        source = piece(own[index], index, chunk, way) if first else target
+        return remote(
+            source,
+            target,
+            send_sems.at[1, index, way, step],
+            recv_sems.at[1, index, way, step],
+            nexts[way],
+        )
+
+    def fan_copy(index, way, step, first):
+        chunk = turned(way, step - 1 + length)
+        target = spot_of(total[index], index, core, chunk, way)
+        source = piece(own[index], index, chunk, way) if first else target
+        return remote(
+            source,
+            target,
+            fan_sems.at[0, index, way, step],
+            fan_sems.at[1, index, way, step],
+            partner,
+        )
+
+    barrier = pltpu.get_barrier_semaphore()
+    for device in (*nexts, partner):
+        pl.semaphore_signal(barrier, inc=1, device_id=device, device_id_type=pl.DeviceIdType.MESH)
+    pl.semaphore_wait(barrier, 3)
+
+    loads = [
+        pltpu.make_async_copy(share(given[index], index, core), own[index], load_sem.at[index])
+        for index in range(count)
+    ]
+    swaps = [
+        remote(
+            share(given[index], index, 1 - core),
+            peer[index],
+            core_sems.at[0, index],
+            core_sems.at[1, index],
+            partner,
+        )
+        for index in range(count)
+    ]
+    for load, swap in zip(loads, swaps):
+        swap.start()
+        load.start()
+    for index in range(count):
+        loads[index].wait()
+        swaps[index].wait_recv()
+        for way in range(2):
+            chunk = turned(way, 0)
+            mine = piece(own[index], index, chunk, way)
+            theirs = piece(peer[index], index, chunk, way)
+            mine[...] = (mine[...].astype(F32) + theirs[...].astype(F32)).astype(mine.dtype)
+            scatter_copy(index, way, 0).start()
+
+    def absorb(index, way, step):
+        scatter_copy(index, way, step - 1).wait_recv()
+        chunk = turned(way, step)
+        mine = piece(own[index], index, chunk, way)
+        theirs = piece(peer[index], index, chunk, way)
+        came = slots[index][way, step - 1]
+        both = mine[...].astype(F32) + theirs[...].astype(F32) + came.astype(F32)
+        mine[...] = both.astype(mine.dtype)
+
+    def scatter_step(step, carry):
+        for index, way in streams:
+            absorb(index, way, step)
+            scatter_copy(index, way, step).start()
+        return carry
+
+    lax.fori_loop(1, length - 1, scatter_step, 0)
+    for index, way in streams:
+        absorb(index, way, length - 1)
+        gather_copy(index, way, 0, True).start()
+        fan_copy(index, way, 0, True).start()
+        chunk = turned(way, length - 1)
+        pltpu.make_async_copy(
+            piece(own[index], index, chunk, way),
+            spot_of(total[index], index, core, chunk, way),
+            keep_sem.at[index, way],
+        ).start()
+
+    def gather_step(step, carry):
+        for index, way in streams:
+            gather_copy(index, way, step - 1, False).wait_recv()
+            gather_copy(index, way, step, False).start()
+            fan_copy(index, way, step, False).start()
+        return carry
+
+    lax.fori_loop(1, length - 1, gather_step, 0)
+    for index, way in streams:
+        gather_copy(index, way, length - 2, False).wait_recv()
+        fan_copy(index, way, length - 1, False).start()
+
+    for index in range(count):
+        swaps[index].wait_send()
+
+    def drain(step, carry):
+        for index, way in streams:
+            scatter_copy(index, way, step).wait_send()
+            gather_copy(index, way, step, False).wait_send()
+            fan_copy(index, way, step, False).wait()
+        return carry
+
+    lax.fori_loop(0, length - 1, drain, 0)
+    for index, way in streams:
+        fan_copy(index, way, length - 1, False).wait()
+        chunk = turned(way, length - 1)
+        pltpu.make_async_copy(
+            piece(own[index], index, chunk, way),
+            spot_of(total[index], index, core, chunk, way),
+            keep_sem.at[index, way],
+        ).wait()
+
+
+def ring_kind(table, length):
+    rows, cols = math.prod(table.shape[:-1]), table.shape[-1]
+    if rows % (length * 4 * 16) == 0 and cols % LANES == 0:
+        return "rows", (length, 2, rows // (2 * length), cols)
+    if rows % (length * 16) == 0 and cols % (4 * LANES) == 0:
+        return "cols", (length, rows // length, cols)
+    return None
+
+
+def ring_sum(tables, small):
+    n_dp = lax.axis_size("dp")
+    length = n_dp // 2
+    cuts = [ring_kind(table, length) for table in tables]
+    if n_dp % 4 or length < 4 or any(cut is None for cut in cuts):
+        return None
+    if small.shape != (32, length * LANES):
+        return None
+    views = [table.reshape(cut[1]) for table, cut in zip(tables, cuts)]
+    views.append(small.reshape(2, 2, 8, small.shape[-1]))
+    kinds = [cut[0] for cut in cuts] + ["small"]
+    own, slots = [], []
+    for view, kind in zip(views, kinds):
+        shape = view.shape
+        if kind == "rows":
+            half = (shape[0], shape[2], shape[3])
+            part = (shape[2] // 2, shape[3])
+        elif kind == "cols":
+            half = (shape[0], shape[1], shape[2] // 2)
+            part = (shape[1], shape[2] // 4)
+        else:
+            half = shape[1:]
+            part = (shape[2], LANES)
+        own.append(pltpu.VMEM(half, view.dtype))
+        slots.append(pltpu.VMEM((2, length - 1, *part), view.dtype))
+    count = len(views)
+    hbm = pl.BlockSpec(memory_space=pl.ANY)
+    moved = sum(view.size * view.dtype.itemsize for view in views)
+    sums = pl.pallas_call(
+        functools.partial(ring_kernel, n_dp, tuple(kinds)),
+        out_shape=tuple(jax.ShapeDtypeStruct(view.shape, view.dtype) for view in views),
+        in_specs=[hbm] * count,
+        out_specs=(hbm,) * count,
+        scratch_shapes=[
+            *own,
+            *own,
+            *slots,
+            pltpu.SemaphoreType.DMA((count,)),
+            pltpu.SemaphoreType.DMA((2, count)),
+            pltpu.SemaphoreType.DMA((2, count, 2, length - 1)),
+            pltpu.SemaphoreType.DMA((2, count, 2, length - 1)),
+            pltpu.SemaphoreType.DMA((2, count, 2, length)),
+            pltpu.SemaphoreType.DMA((count, 2)),
+        ],
+        compiler_params=pltpu.CompilerParams(
+            vmem_limit_bytes=VMEM_LIMIT, collective_id=0, has_side_effects=True
+        ),
+        cost_estimate=pl.CostEstimate(flops=0, bytes_accessed=30 * moved, transcendentals=0),
+        name="ring_sum",
+    )(*views)
+    return [
+        result.reshape(table.shape) for result, table in zip(sums, [*tables, small])
+    ]
 
 
 def body(
@@ -531,7 +797,7 @@
             level, e, hid, adds, norm_gain, *mlp_kept, gate_up_weight, down_weight
         )
         gain_rows[(level + 1, 0)] = rows
-        e, rows, part, grad_qkv, grad_conv, grad_beta, head_rows, grad_out = mixer_backward(
+        e, part, small[level], grad_qkv, grad_out = mixer_backward(
             level,
             e,
             h,
@@ -544,10 +810,8 @@
             qkv_weight,
             out_weight,
         )
-        gain_rows[(level, 1)] = rows
         hid, adds = x, branch_parts(part)
-        small[level] = (grad_conv, grad_beta[:, :heads], head_rows[0])
-        big[level] = (grad_qkv, grad_out, grad_gate_up, grad_down)
+        big[level] = (grad_out, grad_down, grad_qkv, grad_gate_up)
     branch = adds[0].astype(F32)
     for add in adds[1:]:
         branch = branch + add.astype(F32)
@@ -555,19 +819,32 @@
     gain_rows[(0, 0)] = rows
     input_grad = (e + grad_hidden).astype(BF16)
 
-    norm_rows = jnp.stack(
-        [jnp.concatenate([gain_rows[(level, 0)], gain_rows[(level, 1)]]) for level in range(LAYERS)]
+    half = rows.shape[-1] // 2
+    small_all = jnp.concatenate(
+        [
+            small[level].at[3:5, SIDE:].set(gain_rows[(level, 0)].reshape(2, half))
+            for level in range(LAYERS)
+        ]
     )
-    norm_rows = norm_rows / lax.axis_size("tensor")
-    grad_norm, grad_out_gain = lax.psum(
-        (norm_rows, jnp.stack([group[2] for group in small])), ("dp", "tensor")
+    tables = [table for level in reversed(range(LAYERS)) for table in big[level]]
+    sums = ring_sum(tables, small_all)
+    if sums is None:
+        sums = [*sum_over_dp(tables), lax.psum(small_all, "dp")]
+    small_all = sums[-1].reshape(LAYERS, 16, -1)
+    chans = conv_taps.shape[-1]
+    grad_conv = small_all[:, : 3 * KCONV, :chans].reshape(conv_taps.shape)
+    grad_beta = small_all[:, 3 * KCONV : 3 * KCONV + heads].transpose(0, 2, 1)
+    grad_norm = jnp.stack(
+        [
+            small_all[:, 3:5, SIDE:].reshape(LAYERS, -1),
+            small_all[:, 1:3, SIDE:].reshape(LAYERS, -1),
+        ],
+        axis=1,
     )
-    grad_conv, grad_beta = lax.psum(
-        (jnp.stack([group[0] for group in small]), jnp.stack([group[1] for group in small])), "dp"
-    )
-    sums = [sum_over_dp(big[level]) for level in range(LAYERS)]
-    grad_qkv, grad_out, grad_gate_up, grad_down = (
-        jnp.stack([sums[level][index] for level in range(LAYERS)]) for index in range(4)
+    grad_out_gain = small_all[:, 0, SIDE : SIDE + DK]
+    grad_out_gain = sum(branch_parts(grad_out_gain))
+    grad_out, grad_down, grad_qkv, grad_gate_up = (
+        jnp.stack([sums[4 + index], sums[index]]).astype(F32) for index in range(4)
     )
     return (
         outputs,

time: 1090 us -> 505 us (0.46)
  waiting for transfers between devices: 650 us -> 73.9 us
  Pallas kernels: 102 us -> 361 us
  local copies, waits for them, and re-layouts: 149 us -> 14.3 us
  other arithmetic: 107 us -> 33.3 us
  blocking collectives: 43.3 us -> 0 us
  between operations: 15.2 us -> 1.11 us
    unnamed x5 -> x0, waiting for transfers between devices: 448 us -> none
    pallas_call x0 -> x1, Pallas kernels: none -> 259 us  [ring_sum(): pl.pallas_call(functools.partial(ring_kernel, n_dp, tuple(kinds)), out_sh...]
    all_gather x2 -> x0, waiting for transfers between devices: 126 us -> none  [sum_over_dp(): joined = lax.all_gather(shard, 'dp', axis=0, tiled=True).astype(F32)]
    another operation x12 -> x4, local copies, waits for them, and re-layouts: 60.2 us -> 0.05 us  [the longest x2 0.04 us: body(): jnp.stack([small_all[:, 3:5, SIDE:].reshape(LAYERS, -1), small_all[:, 1:3...]
    concatenate x1, other arithmetic: 58.6 us -> 1.5 us  [body(): jnp.concatenate([small[level].at[3:5, SIDE:].set(gain_rows[level, 0].resh...]
    another operation x9 -> x1, other arithmetic: 43.5 us -> 0.01 us  [body(): jnp.stack([small_all[:, 3:5, SIDE:].reshape(LAYERS, -1), small_all[:, 1:3...]
    psum x1 -> x0, blocking collectives: 43.3 us -> none  [body(): lax.psum((norm_rows, jnp.stack([group[2] for group in small])), ('dp', 't...]
    slice x8 -> x4, local copies, waits for them, and re-layouts: 33.5 us -> 1.58 us  [the longest x1 0.84 us: body(): small_all[:, 3:5, SIDE:].reshape(LAYERS, -1)]
  transfers between devices with their start and end apart: 12 -> 9, of which waited for: 10 -> 7; matrix products, arithmetic and copies ran while one was open for 17% -> 6% of each run, Pallas kernels for 0% -> 3%
where the time goes in v2:
time: 505 us; the launch traced here: 496 us
  Pallas kernels  361 us (71%)
  waiting for transfers between devices  73.9 us (15%)
  other arithmetic  33.3 us (7%)
  local copies, waits for them, and re-layouts  14.3 us (3%)
  starting transfers between devices  12.5 us (2%)
    pallas_call x1, Pallas kernels, ring_sum(): pl.pallas_call(functools.partial(ring_kernel, n_dp, tuple(kinds)), out_sh...  259 us
    ppermute x9, waiting for transfers between devices, branch_parts(): return (part, lax.ppermute(part, 'tensor', [(0, 1), (1, 0)]))  73.9 us
    pallas_call x2, Pallas kernels, mixer_forward(): pl.pallas_call(functools.partial(mixer_forward_kernel, level, heads, len(...  30.3 us
    pallas_call x2, Pallas kernels, mixer_backward(): pl.pallas_call(functools.partial(mixer_backward_kernel, level, heads, len...  29.1 us
    convert_element_type x4, other arithmetic, body(): jnp.stack([sums[4 + index], sums[index]]).astype(F32)  26.8 us
    pallas_call x2, Pallas kernels, mlp_backward(): pl.pallas_call(functools.partial(mlp_backward_kernel, level, len(adds)),...  26.3 us
    pallas_call x2, Pallas kernels, mlp_forward(): pl.pallas_call(functools.partial(mlp_forward_kernel, level, len(adds)), o...  15.9 us
    ppermute x9, starting transfers between devices, branch_parts(): return (part, lax.ppermute(part, 'tensor', [(0, 1), (1, 0)]))  12.5 us
  transfers between devices with their start and end apart: 9, of which 7 were waited for; matrix products, arithmetic and copies ran while one was open for 6% of the time, Pallas kernels for 3%

profile of v2, /device:TPU:0, one launch (start us, length us, event | category | flops | bytes accessed | tf_op | source)
XLA Modules:
  0.0 496.1 jit_solution(7344055375709699557)
XLA Ops:
  2.6 14.9 %mixer_forward.2 = (f32[256,1024]{1,0:T(8,128)}, bf16[256,1024]{1,0:T(8,128)(2,1)}, f32[3,256,512]{2,1,0:T(8,128)}, f32[256,128]{1,0:T(8,128)}, bf16[2,4,256,256...) custom-call(bf16[256,1024]{1,0:T(8,128)(2,1)} %refs_0_.2, ...), custom_call_target="tpu_custom_call" | custom-call | tf_op jit(solution)/shard_map/mixer_forward/pallas_call | solution.py:188
  17.5 3.0 collective-permute-start
  20.5 12.1 %collective-permute-done.refs_2_ = bf16[256,1024]{1,0:T(8,128)(2,1)S(1)} collective-permute-done((bf16[256,1024]{1,0:T(8,128)(2,1)}, bf16[256,1024]{1,0:T(8,128)(2,1)S(1)}, u32[]{:S(2)}, u32[]{:S(2)}) %collective-permute-start) | collective-permute-done | bytes 524320 | tf_op jit(solution)/shard_map/ppermute | solution.py:475
  33.4 7.9 %mlp_forward.2 = (f32[256,1024]{1,0:T(8,128)}, bf16[256,1024]{1,0:T(8,128)(2,1)}, f32[2,256,1408]{2,1,0:T(8,128)}, bf16[256,1408]{1,0:T(8,128)(2,1)}, bf16[256,1024]{1,0:T(8,128)(2,1)}) custom-call(f32[256,1024]{1,0:T(8,128)} %get-tuple-element.90.refs_0_, bf16[256,1024]{1,0:T(8,128)(2,1)} %get-tuple-element.91.refs_1_, bf16[256,1024]{1,0:T(8,128)(2,1)} %copy-done.14, ...), custom_call_target="tpu_custom_call" | custom-call | tf_op jit(solution)/shard_map/mlp_forward/pallas_call | solution.py:249
  41.3 1.8 collective-permute-start.1
  43.1 11.6 %collective-permute-done.1.refs_2_ = bf16[256,1024]{1,0:T(8,128)(2,1)S(1)} collective-permute-done((bf16[256,1024]{1,0:T(8,128)(2,1)}, bf16[256,1024]{1,0:T(8,128)(2,1)S(1)}, u32[]{:S(2)}, u32[]{:S(2)}) %collective-permute-start.1) | collective-permute-done | bytes 524320 | tf_op jit(solution)/shard_map/ppermute | solution.py:475
  55.5 15.4 %mixer_forward.3 = (f32[256,1024]{1,0:T(8,128)}, bf16[256,1024]{1,0:T(8,128)(2,1)}, f32[3,256,512]{2,1,0:T(8,128)}, f32[256,128]{1,0:T(8,128)}, bf16[2,4,256,256...) custom-call(f32[256,1024]{1,0:T(8,128)} %get-tuple-element.92.refs_0, ...), custom_call_target="tpu_custom_call" | custom-call | tf_op jit(solution)/shard_map/mixer_forward/pallas_call | solution.py:188
  70.9 1.5 collective-permute-start.2
  72.3 11.0 %collective-permute-done.2.refs_2_ = bf16[256,1024]{1,0:T(8,128)(2,1)S(1)} collective-permute-done((bf16[256,1024]{1,0:T(8,128)(2,1)}, bf16[256,1024]{1,0:T(8,128)(2,1)S(1)}, u32[]{:S(2)}, u32[]{:S(2)}) %collective-permute-start.2) | collective-permute-done | bytes 524320 | tf_op jit(solution)/shard_map/ppermute | solution.py:475
  84.1 8.1 %mlp_forward.3 = (f32[256,1024]{1,0:T(8,128)}, bf16[256,1024]{1,0:T(8,128)(2,1)}, f32[2,256,1408]{2,1,0:T(8,128)}, bf16[256,1408]{1,0:T(8,128)(2,1)}, bf16[256,1024]{1,0:T(8,128)(2,1)}) custom-call(f32[256,1024]{1,0:T(8,128)} %get-tuple-element.94.refs_0_.refs_1_, bf16[256,1024]{1,0:T(8,128)(2,1)} %get-tuple-element.95.refs_1_, ...), custom_call_target="tpu_custom_call" | custom-call | tf_op jit(solution)/shard_map/mlp_forward/pallas_call | solution.py:249
  92.2 12.9 %mlp_backward.2 = (f32[256,1024]{1,0:T(8,128)}, f32[1,1024]{1,0:T(1,128)}, bf16[256,1024]{1,0:T(8,128)(2,1)}, bf16[1408,1024]{1,0:T(8,128)(2,1)}, bf16[2,1024,1408]{2,1,0:T(8,128)(2,1)}) custom-call(bf16[256,1024]{1,0:T(8,128)(2,1)} %refs_0_.3, f32[256,1024]{1,0:T(8,128)} %get-tuple-element.94.refs_0_.refs_1_, bf16[2,2,1024]{2,1,0:T(2,128)(2,1)} %refs_4_.11, ...), custom_call_target="tpu_custom_call" | custom-call | tf_op jit(solution)/shard_map/mlp_backward/pallas_call | solution.py:317
  105.1 1.1 collective-permute-start.4
  106.3 10.4 %collective-permute-done.4.refs_3_ = bf16[256,1024]{1,0:T(8,128)(2,1)S(1)} collective-permute-done((bf16[256,1024]{1,0:T(8,128)(2,1)}, bf16[256,1024]{1,0:T(8,128)(2,1)S(1)}, u32[]{:S(2)}, u32[]{:S(2)}) %collective-permute-start.4) | collective-permute-done | bytes 524320 | tf_op jit(solution)/shard_map/ppermute | solution.py:475
  117.5 14.6 %mixer_backward.2 = (f32[256,1024]{1,0:T(8,128)}, bf16[256,1024]{1,0:T(8,128)(2,1)}, f32[16,1024]{1,0:T(8,128)}, bf16[3,1024,512]{2,1,0:T(8,128)(2,1)}, bf16[512,1024]{1,0:T(8,128)(2,1)}) custom-call(f32[256,1024]{1,0:T(8,128)} %get-tuple-element.101.refs_0_, f32[256,1024]{1,0:T(8,128)} %get-tuple-element.96.refs_1_, ...), custom_call_target="tpu_custom_call" | custom-call | tf_op jit(solution)/shard_map/mixer_backward/pallas_call | solution.py:446
  132.9 9.8 %collective-permute-done.5.refs_3_ = bf16[256,1024]{1,0:T(8,128)(2,1)S(1)} collective-permute-done((bf16[256,1024]{1,0:T(8,128)(2,1)}, bf16[256,1024]{1,0:T(8,128)(2,1)S(1)}, u32[]{:S(2)}, u32[]{:S(2)}) %collective-permute-start.5) | collective-permute-done | bytes 524320 | tf_op jit(solution)/shard_map/ppermute | solution.py:475
  143.5 13.4 %mlp_backward.3 = (f32[256,1024]{1,0:T(8,128)}, f32[1,1024]{1,0:T(1,128)}, bf16[256,1024]{1,0:T(8,128)(2,1)}, bf16[1408,1024]{1,0:T(8,128)(2,1)}, bf16[2,1024,1408]{2,1,0:T(8,128)(2,1)}) custom-call(f32[256,1024]{1,0:T(8,128)} %get-tuple-element.110.refs_0_, f32[256,1024]{1,0:T(8,128)} %get-tuple-element.94.refs_0_.refs_1_, ...), custom_call_target="tpu_custom_call" | custom-call | tf_op jit(solution)/shard_map/mlp_backward/pallas_call | solution.py:317
  157.5 1.6 collective-permute-start.3
  159.2 12.9 %collective-permute-done.6.refs_3_ = bf16[256,1024]{1,0:T(8,128)(2,1)S(1)} collective-permute-done((bf16[256,1024]{1,0:T(8,128)(2,1)}, bf16[256,1024]{1,0:T(8,128)(2,1)S(1)}, u32[]{:S(2)}, u32[]{:S(2)}) %collective-permute-start.6) | collective-permute-done | bytes 524320 | tf_op jit(solution)/shard_map/ppermute | solution.py:475
  173.0 14.4 %mixer_backward.3 = (f32[256,1024]{1,0:T(8,128)}, bf16[256,1024]{1,0:T(8,128)(2,1)}, f32[16,1024]{1,0:T(8,128)}, bf16[3,1024,512]{2,1,0:T(8,128)(2,1)}, bf16[512,1024]{1,0:T(8,128)(2,1)}) custom-call(f32[256,1024]{1,0:T(8,128)} %get-tuple-element.115.refs_0_, f32[256,1024]{1,0:T(8,128)} %get-tuple-element.92.refs_0_.refs_1_, ...), custom_call_target="tpu_custom_call" | custom-call | tf_op jit(solution)/shard_map/mixer_backward/pallas_call | solution.py:446
  188.0 1.0 add_convert_fusion.1
  190.7 6.2 %collective-permute-done.7 = bf16[256,1024]{1,0:T(8,128)(2,1)S(1)} collective-permute-done((bf16[256,1024]{1,0:T(8,128)(2,1)}, bf16[256,1024]{1,0:T(8,128)(2,1)S(1)}, u32[]{:S(2)}, u32[]{:S(2)}) %collective-permute-start.7) | collective-permute-done | bytes 524320 | tf_op jit(solution)/shard_map/ppermute | solution.py:475
  196.9 1.4 multiply_reduce_fusion
  198.3 2.1 scatter.6
  200.4 1.5 pad_maximum_fusion
  201.9 259.3 %ring_sum.1 = (bf16[8,2,32,1024]{3,2,1,0:T(8,128)(2,1)}, bf16[8,176,1024]{2,1,0:T(8,128)(2,1)}, bf16[8,2,192,512]{3,2,1,0:T(8,128)(2,1)}, bf16[8,2,128,1408]{3,2...) custom-call(bf16[8,2,32,1024]{3,2,1,0:T(8,128)(2,1)} %bitcast.41, ...), custom_call_target="tpu_custom_call" | custom-call | bytes 774635520 | tf_op jit(solution)/shard_map/ring_sum/pallas_call | solution.py:733
  461.2 1.5 slice_bitcast_fusion
  464.2 1.6 collective-permute-start.8
  465.9 10.2 %maximum_convert_fusion.1 = f32[2,3,1024,512]{3,2,1,0:T(8,128)} fusion(bf16[1,3,1024,512]{3,2,1,0:T(8,128)(2,1)} %bitcast.35, bf16[1,3,1024,512]{3,2,1,0:T(8,128)(2,1)} %bitcast.36), kind=kLoop, calls=%fused_computation.1 | loop fusion | flops 6291456 | bytes 18874368 | tf_op jit(solution)/shard_map/convert_element_type | solution.py:847
  476.1 2.3 maximum_convert_fusion.3
  478.4 9.2 %maximum_convert_fusion = f32[2,2,1024,1408]{3,2,1,0:T(8,128)} fusion(bf16[1,2,1024,1408]{3,2,1,0:T(8,128)(2,1)S(1)} %bitcast.29, bf16[1,2,1024,1408]{3,2,1,0:T(8,128)(2,1)S(1)} %bitcast.32), kind=kLoop, calls=%fused_computation | loop fusion | flops 11534336 | bytes 34603008 | tf_op jit(solution)/shard_map/convert_element_type | solution.py:847
  487.6 5.2 %maximum_convert_fusion.2 = f32[2,1408,1024]{2,1,0:T(8,128)} fusion(bf16[1,1408,1024]{2,1,0:T(8,128)(2,1)S(1)} %bitcast.39, bf16[1,1408,1024]{2,1,0:T(8,128)(2,1)S(1)} %bitcast.40), kind=kLoop, calls=%fused_computation.2 | loop fusion | flops 5767168 | bytes 17301504 | tf_op jit(solution)/shard_map/convert_element_type | solution.py:847
  492.8 1.2 add_convert_fusion
  (74 shorter events, 14.0 us)
Async XLA Ops:
  17.5 15.1 %collective-permute-start = (bf16[256,1024]{1,0:T(8,128)(2,1)}, bf16[256,1024]{1,0:T(8,128)(2,1)S(1)}, u32[]{:S(2)}, u32[]{:S(2)}) collective-permute-start(bf16[256,1024]{1,0:T(8,128)(2,1)} %get-tuple-element.91.refs_1_), channel_id=1, source_target_pairs={{0,1},{1,0},{2,3},{3,2},{4,5},{5,4},{6,7},{7,6},{8,9},{9,8},{10,11... | collective-permute-start | bytes 1572872 | tf_op jit(solution)/shard_map/ppermute | solution.py:475
  32.6 0.8 copy-start.14
  41.3 13.4 %collective-permute-start.1 = (bf16[256,1024]{1,0:T(8,128)(2,1)}, bf16[256,1024]{1,0:T(8,128)(2,1)S(1)}, u32[]{:S(2)}, u32[]{:S(2)}) collective-permute-start(bf16[256,1024]{1,0:T(8,128)(2,1)} %get-tuple-element.93.refs_1_), channel_id=1, source_target_pairs={{0,1},{1,0},{2,3},{3,2},{4,5},{5,4},{6,7},{7,6},{8,9},{9,8},{10,11... | collective-permute-start | bytes 1572872 | tf_op jit(solution)/shard_map/ppermute | solution.py:475
  54.7 0.8 copy-start.13
  70.9 12.5 %collective-permute-start.2 = (bf16[256,1024]{1,0:T(8,128)(2,1)}, bf16[256,1024]{1,0:T(8,128)(2,1)S(1)}, u32[]{:S(2)}, u32[]{:S(2)}) collective-permute-start(bf16[256,1024]{1,0:T(8,128)(2,1)} %get-tuple-element.95.refs_1_), channel_id=1, source_target_pairs={{0,1},{1,0},{2,3},{3,2},{4,5},{5,4},{6,7},{7,6},{8,9},{9,8},{10,11... | collective-permute-start | bytes 1572872 | tf_op jit(solution)/shard_map/ppermute | solution.py:475
  83.3 0.8 copy-start.15
  105.1 11.5 %collective-permute-start.4 = (bf16[256,1024]{1,0:T(8,128)(2,1)}, bf16[256,1024]{1,0:T(8,128)(2,1)S(1)}, u32[]{:S(2)}, u32[]{:S(2)}) collective-permute-start(bf16[256,1024]{1,0:T(8,128)(2,1)} %get-tuple-element.102.refs_2_), channel_id=1, source_target_pairs={{0,1},{1,0},{2,3},{3,2},{4,5},{5,4},{6,7},{7,6},{8,9},{9,8},{10,11... | collective-permute-start | bytes 1572872 | tf_op jit(solution)/shard_map/ppermute | solution.py:475
  116.7 0.8 copy-start.11
  132.1 10.6 %collective-permute-start.5 = (bf16[256,1024]{1,0:T(8,128)(2,1)}, bf16[256,1024]{1,0:T(8,128)(2,1)S(1)}, u32[]{:S(2)}, u32[]{:S(2)}) collective-permute-start(bf16[256,1024]{1,0:T(8,128)(2,1)} %get-tuple-element.111.refs_2_), channel_id=1, source_target_pairs={{0,1},{1,0},{2,3},{3,2},{4,5},{5,4},{6,7},{7,6},{8,9},{9,8},{10,11... | collective-permute-start | bytes 1572872 | tf_op jit(solution)/shard_map/ppermute | solution.py:475
  142.7 0.8 copy-start.12
  143.5 14.0 %copy-start.9 = (bf16[256,1024]{1,0:T(8,128)(2,1)S(1)}, bf16[256,1024]{1,0:T(8,128)(2,1)}, u32[]{:S(2)}) copy-start(bf16[256,1024]{1,0:T(8,128)(2,1)} %get-tuple-element.97) | copy-start | bytes 1572868
  143.5 15.6 %copy-start = (f32[256,1024]{1,0:T(8,128)S(1)}, f32[256,1024]{1,0:T(8,128)}, u32[]{:S(2)}) copy-start(f32[256,1024]{1,0:T(8,128)} %get-tuple-element.90.refs_0_) | copy-start | bytes 3145732
  157.0 15.1 %collective-permute-start.6 = (bf16[256,1024]{1,0:T(8,128)(2,1)}, bf16[256,1024]{1,0:T(8,128)(2,1)S(1)}, u32[]{:S(2)}, u32[]{:S(2)}) collective-permute-start(bf16[256,1024]{1,0:T(8,128)(2,1)} %get-tuple-element.116.refs_2_), channel_id=1, source_target_pairs={{0,1},{1,0},{2,3},{3,2},{4,5},{5,4},{6,7},{7,6},{8,9},{9,8},{10,11... | collective-permute-start | bytes 1572872 | tf_op jit(solution)/shard_map/ppermute | solution.py:475
  157.5 30.5 %collective-permute-start.3 = (bf16[256,1024]{1,0:T(8,128)(2,1)S(1)}, bf16[256,1024]{1,0:T(8,128)(2,1)S(1)}, u32[]{:S(2)}, u32[]{:S(2)}) collective-permute-start(bf16[256,1024]{1,0:T(8,128)(2,1)S(1)} %copy-done.9), channel_id=1, source_target_pairs={{0,1},{1,0},{2,3},{3,2},{4,5},{5,4},{6,7},{7,6},{8,9},{9,8},{10,11... | collective-permute-start | bytes 1572872 | tf_op jit(solution)/shard_map/ppermute | solution.py:475
  172.1 0.9 copy-start.10
  173.0 15.0 %copy-start.8 = (bf16[2,2,1024]{2,1,0:T(2,128)(2,1)S(1)}, bf16[2,2,1024]{2,1,0:T(2,128)(2,1)}, u32[]{:S(2)}) copy-start(bf16[2,2,1024]{2,1,0:T(2,128)(2,1)} %refs_4_.11) | copy-start | bytes 24580
  173.0 15.0 %copy-start.1 = (f32[256,1024]{1,0:T(8,128)S(1)}, f32[256,1024]{1,0:T(8,128)}, u32[]{:S(2)}) copy-start(f32[256,1024]{1,0:T(8,128)} %get-tuple-element.96.refs_1_) | copy-start | bytes 3145732
  173.0 16.6 %copy-start.18 = (f32[1,1024]{1,0:T(1,128)S(1)}, f32[1,1024]{1,0:T(1,128)}, u32[]{:S(2)}) copy-start(f32[1,1024]{1,0:T(1,128)} %get-tuple-element.136) | copy-start | bytes 12292
  173.0 17.2 %copy-start.17 = (f32[16,1024]{1,0:T(8,128)S(1)}, f32[16,1024]{1,0:T(8,128)}, u32[]{:S(2)}) copy-start(f32[16,1024]{1,0:T(8,128)} %get-tuple-element.135) | copy-start | bytes 196612
  187.4 9.5 %collective-permute-start.7 = (bf16[256,1024]{1,0:T(8,128)(2,1)}, bf16[256,1024]{1,0:T(8,128)(2,1)S(1)}, u32[]{:S(2)}, u32[]{:S(2)}) collective-permute-start(bf16[256,1024]{1,0:T(8,128)(2,1)} %get-tuple-element.125), channel_id=1, source_target_pairs={{0,1},{1,0},{2,3},{3,2},{4,5},{5,4},{6,7},{7,6},{8,9},{9,8},{10,11... | collective-permute-start | bytes 1572872 | tf_op jit(solution)/shard_map/ppermute | solution.py:475
  464.2 31.1 %collective-permute-start.8 = (f32[2,128]{1,0:T(2,128)S(1)}, f32[2,128]{1,0:T(2,128)S(1)}, u32[]{:S(2)}, u32[]{:S(2)}) collective-permute-start(f32[2,128]{1,0:T(2,128)S(1)} %bitcast.53), channel_id=1, source_target_pairs={{0,1},{1,0},{2,3},{3,2},{4,5},{5,4},{6,7},{7,6},{8,9},{9,8},{10,11... | collective-permute-start | bytes 3080 | tf_op jit(solution)/shard_map/ppermute | solution.py:475
  465.8 12.5 %slice-start = ((s8[5767168]{0:T(1024)(128)(4,1)}), s8[4194304]{0:T(1024)(128)(4,1)S(1)}, s32[]{:S(2)}) async-start(s8[5767168]{0:T(1024)(128)(4,1)} %bitcast.27), calls=%async_computation | async-start | bytes 8388608
  465.8 12.5 %slice-start.2 = ((s8[5767168]{0:T(1024)(128)(4,1)}), s8[4194304]{0:T(1024)(128)(4,1)S(1)}, s32[]{:S(2)}) async-start(s8[5767168]{0:T(1024)(128)(4,1)} %bitcast.30), calls=%async_computation.2 | async-start | bytes 8388608
  465.9 10.2 %copy-start.6 = (bf16[8,2,32,1024]{3,2,1,0:T(8,128)(2,1)S(1)}, bf16[8,2,32,1024]{3,2,1,0:T(8,128)(2,1)}, u32[]{:S(2)}) copy-start(bf16[8,2,32,1024]{3,2,1,0:T(8,128)(2,1)} %get-tuple-element.141) | copy-start | bytes 3145732
  465.9 10.2 %copy-start.7 = (bf16[8,2,32,1024]{3,2,1,0:T(8,128)(2,1)S(1)}, bf16[8,2,32,1024]{3,2,1,0:T(8,128)(2,1)}, u32[]{:S(2)}) copy-start(bf16[8,2,32,1024]{3,2,1,0:T(8,128)(2,1)} %get-tuple-element.140) | copy-start | bytes 3145732
  465.9 12.5 %slice-start.1 = ((s8[5767168]{0:T(1024)(128)(4,1)}), s8[1572864]{0:T(1024)(128)(4,1)S(1)}, s32[]{:S(2)}) async-start(s8[5767168]{0:T(1024)(128)(4,1)} %bitcast.27), calls=%async_computation.1 | async-start | bytes 3145728
  465.9 12.5 %slice-start.3 = ((s8[5767168]{0:T(1024)(128)(4,1)}), s8[1572864]{0:T(1024)(128)(4,1)S(1)}, s32[]{:S(2)}) async-start(s8[5767168]{0:T(1024)(128)(4,1)} %bitcast.30), calls=%async_computation.3 | async-start | bytes 3145728
  478.4 9.2 %copy-start.2 = (bf16[8,176,1024]{2,1,0:T(8,128)(2,1)S(1)}, bf16[8,176,1024]{2,1,0:T(8,128)(2,1)}, u32[]{:S(2)}) copy-start(bf16[8,176,1024]{2,1,0:T(8,128)(2,1)} %get-tuple-element.145) | copy-start | bytes 8650756
  478.4 9.2 %copy-start.3 = (bf16[8,176,1024]{2,1,0:T(8,128)(2,1)S(1)}, bf16[8,176,1024]{2,1,0:T(8,128)(2,1)}, u32[]{:S(2)}) copy-start(bf16[8,176,1024]{2,1,0:T(8,128)(2,1)} %get-tuple-element.144) | copy-start | bytes 8650756
  487.6 5.2 %copy-start.4 = (bf16[256,1024]{1,0:T(8,128)(2,1)S(1)}, bf16[256,1024]{1,0:T(8,128)(2,1)}, u32[]{:S(2)}) copy-start(bf16[256,1024]{1,0:T(8,128)(2,1)} %get-tuple-element.125) | copy-start | bytes 1572868
  487.6 5.2 %copy-start.5 = (f32[256,1024]{1,0:T(8,128)S(1)}, f32[256,1024]{1,0:T(8,128)}, u32[]{:S(2)}) copy-start(f32[256,1024]{1,0:T(8,128)} %get-tuple-element.124) | copy-start | bytes 3145732
  487.6 6.4 %copy-start.16 = (f32[2,2,8,1024]{3,2,1,0:T(8,128)S(1)}, f32[2,2,8,1024]{3,2,1,0:T(8,128)}, u32[]{:S(2)}) copy-start(f32[2,2,8,1024]{3,2,1,0:T(8,128)} %get-tuple-element.139) | copy-start | bytes 393220

commit v3 on v2

--- a/solution.py
+++ b/solution.py
@@ -119,152 +119,233 @@
     return slice(head * DK, (head + 1) * DK)
 
 
-def mixer_forward_kernel(level, heads, n_add, *refs):
-    (x_ref, *adds) = refs[: 1 + n_add]
-    (gain_ref, taps_ref, head_gain_ref, wb_ref, wq_hbm, wo_hbm) = refs[1 + n_add : 7 + n_add]
-    (x_out, n1_out, p_out, logit_out, t_out, u_out, o_out, on_out, part_out) = refs[
-        7 + n_add : 16 + n_add
+KEPT = ("x", "n1", "p", "logits", "t", "u", "o", "on", "h", "n2", "gu", "z")
+
+
+def kept_shapes(length, width, chans, hidden):
+    heads = chans // DK
+    shapes = dict(
+        x=((length, width), F32),
+        n1=((length, width), BF16),
+        p=((3, length, chans), F32),
+        logits=((length, LANES), F32),
+        t=((2, heads, length, length), BF16),
+        u=((length, chans), BF16),
+        o=((length, chans), F32),
+        on=((length, chans), BF16),
+        h=((length, width), F32),
+        n2=((length, width), BF16),
+        gu=((2, length, hidden), F32),
+        z=((length, hidden), BF16),
+    )
+    return [((LAYERS, *shapes[name][0]), shapes[name][1]) for name in KEPT]
+
+
+class Exchange:
+    def __init__(self, slots, send_sems, recv_sems):
+        self.slots, self.send_sems, self.recv_sems = slots, send_sems, recv_sems
+        self.count = slots.shape[1]
+        self.me = lax.axis_index("tensor")
+        self.pending = []
+
+    def greet(self):
+        barrier = pltpu.get_barrier_semaphore()
+        for away in range(1, self.count):
+            pl.semaphore_signal(
+                barrier,
+                inc=1,
+                device_id={"tensor": lax.rem(self.me + away, self.count)},
+                device_id_type=pl.DeviceIdType.MESH,
+            )
+        pl.semaphore_wait(barrier, self.count - 1)
+
+    def copies(self, spot, part, rows):
+        mine = self.slots.at[spot, self.me, rows]
+        return [
+            pltpu.make_async_remote_copy(
+                src_ref=mine,
+                dst_ref=mine,
+                send_sem=self.send_sems.at[spot, part, away - 1],
+                recv_sem=self.recv_sems.at[spot, part, away - 1],
+                device_id={"tensor": lax.rem(self.me + away, self.count)},
+                device_id_type=pl.DeviceIdType.MESH,
+            )
+            for away in range(1, self.count)
+        ]
+
+    def give(self, spot, part, rows, value):
+        self.slots[spot, self.me, rows] = value
+        for copy in self.copies(spot, part, rows):
+            copy.start()
+            self.pending.append(copy)
+
+    def take(self, spot, part, rows):
+        for copy in self.copies(spot, part, rows):
+            copy.wait_recv()
+        total = self.slots[spot, 0, rows].astype(F32)
+        for index in range(1, self.count):
+            total = total + self.slots[spot, index, rows].astype(F32)
+        return total
+
+    def finish(self):
+        for copy in self.pending:
+            copy.wait_send()
+
+
+def forward_kernel(n_parts, *refs):
+    (x_ref, gain_ref, taps_ref, head_gain_ref, wb_ref) = refs[:5]
+    (wq_hbm, wo_hbm, wgu_hbm, wd_hbm) = refs[5:9]
+    count = len(KEPT)
+    outs = dict(zip(KEPT, refs[9 : 9 + count]))
+    last_out = refs[9 + count]
+    held = dict(zip(KEPT, refs[10 + count : 10 + 2 * count]))
+    (wq, wo, wgu, wd, slots, last, load_sems, keep_sems, send_sems, recv_sems) = refs[
+        10 + 2 * count :
     ]
-    wq, wo, sems = refs[16 + n_add :]
+    exchange = Exchange(slots, send_sems, recv_sems)
+    sources = ((wq_hbm, wq), (wo_hbm, wo), (wgu_hbm, wgu), (wd_hbm, wd))
     loads = [
-        pltpu.make_async_copy(wq_hbm.at[level], wq, sems.at[0]),
-        pltpu.make_async_copy(wo_hbm.at[level], wo, sems.at[1]),
+        [
+            pltpu.make_async_copy(source.at[level], target.at[level], load_sems.at[level, index])
+            for index, (source, target) in enumerate(sources)
+        ]
+        for level in range(LAYERS)
     ]
-    for load in loads:
-        load.start()
-    x = x_ref[...].astype(F32)
-    for add in adds:
-        x = x + add[...].astype(F32)
-    x_out[...] = x
-    length = x.shape[0]
-    n1 = low(x * rms_scale(x) * gain_ref[level, 0:1, :].astype(F32))
-    n1_out[...] = n1
-    logits = dot_nn(n1, wb_ref[level])
-    logit_out[...] = logits
-    beta = sigmoid(logits)
-    loads[0].wait()
-    acts = []
-    for part in range(3):
-        p = dot_nn(n1, wq[part])
-        p_out[part] = p
-        acts.append(conv_silu(p, taps_ref[level, part].astype(F32))[2])
+    for group in loads:
+        for load in group:
+            load.start()
+    exchange.greet()
+    keeps = []
+
+    def keep(name, level):
+        copy = pltpu.make_async_copy(
+            held[name].at[level], outs[name].at[level], keep_sems.at[KEPT.index(name), level]
+        )
+        copy.start()
+        keeps.append(copy)
+
+    length = x_ref.shape[0]
+    heads = wo.shape[1] // DK
+    high = length // n_parts
+    parts = [(part, slice(part * high, (part + 1) * high)) for part in range(n_parts)]
     row, col = positions(length)
-    lowers, scores, values = [], [], []
-    for head in range(heads):
-        cols = head_cols(head)
-        c0, c1, c2 = (act[:, cols] for act in acts)
-        q = low(c0 * lax.rsqrt(jnp.sum(c0 * c0, axis=-1, keepdims=True) + 0.001))
-        k = low(c1 * lax.rsqrt(jnp.sum(c1 * c1, axis=-1, keepdims=True) + 0.001))
-        v = low(c2).astype(F32)
-        gate = beta[:, head : head + 1]
-        lowers.append(jnp.where(row > col, gate * dot_nt(k, k), 0.0))
-        scores.append(low(jnp.where(row >= col, dot_nt(q, k), 0.0)))
-        values.append(halves(gate * v))
-    inverse = unit_lower_inverse(lowers)
-    head_gain = head_gain_ref[level : level + 1, :].astype(F32)
-    for head in range(heads):
-        cols = head_cols(head)
-        t_hi, t_lo = halves(inverse[head])
-        t_out[0, head] = t_hi
-        t_out[1, head] = t_lo
-        u = split_dot(dot_nn, (t_hi, t_lo), values[head])
-        u_low = low(u)
-        u_out[:, cols] = u_low
-        o = dot_nn(scores[head], u_low)
-        o_out[:, cols] = o
-        scale = lax.rsqrt(jnp.mean(o * o, axis=-1, keepdims=True) + 0.01)
-        on_out[:, cols] = low(o * scale * head_gain)
-    loads[1].wait()
-    part_out[...] = low(dot_nn(on_out[...], wo[...]))
-
-
-def mixer_forward(level, x, adds, norm_gain, taps, head_gain, wb, wq, wo):
+    for level in range(LAYERS):
+        for part, rows in parts:
+            if level == 0:
+                x = x_ref[rows].astype(F32)
+            else:
+                x = held["h"][level - 1, rows] + exchange.take(2 * level - 1, part, rows)
+            held["x"][level, rows] = x
+            n1 = low(x * rms_scale(x) * gain_ref[level, 0:1, :].astype(F32))
+            held["n1"][level, rows] = n1
+            held["logits"][level, rows] = dot_nn(n1, wb_ref[level])
+            if part == 0:
+                loads[level][0].wait()
+            for index in range(3):
+                held["p"][level, index, rows] = dot_nn(n1, wq[level, index])
+        for name in ("x", "n1", "logits", "p"):
+            keep(name, level)
+        beta = sigmoid(held["logits"][level])
+        acts = [
+            conv_silu(held["p"][level, index], taps_ref[level, index].astype(F32))[2]
+            for index in range(3)
+        ]
+        lowers, scores, values = [], [], []
+        for head in range(heads):
+            cols = head_cols(head)
+            c0, c1, c2 = (act[:, cols] for act in acts)
+            q = low(c0 * lax.rsqrt(jnp.sum(c0 * c0, axis=-1, keepdims=True) + 0.001))
+            k = low(c1 * lax.rsqrt(jnp.sum(c1 * c1, axis=-1, keepdims=True) + 0.001))
+            v = low(c2).astype(F32)
+            gate = beta[:, head : head + 1]
+            lowers.append(jnp.where(row > col, gate * dot_nt(k, k), 0.0))
+            scores.append(low(jnp.where(row >= col, dot_nt(q, k), 0.0)))
+            values.append(halves(gate * v))
+        inverse = unit_lower_inverse(lowers)
+        head_gain = head_gain_ref[level : level + 1, :].astype(F32)
+        for head in range(heads):
+            cols = head_cols(head)
+            t_hi, t_lo = halves(inverse[head])
+            held["t"][level, 0, head] = t_hi
+            held["t"][level, 1, head] = t_lo
+            u_low = low(split_dot(dot_nn, (t_hi, t_lo), values[head]))
+            held["u"][level, :, cols] = u_low
+            o = dot_nn(scores[head], u_low)
+            held["o"][level, :, cols] = o
+            scale = lax.rsqrt(jnp.mean(o * o, axis=-1, keepdims=True) + 0.01)
+            held["on"][level, :, cols] = low(o * scale * head_gain)
+        loads[level][1].wait()
+        for part, rows in parts:
+            out = dot_nn(held["on"][level, rows], wo[level])
+            exchange.give(2 * level, part, rows, low(out))
+        for name in ("t", "u", "o", "on"):
+            keep(name, level)
+        for part, rows in parts:
+            h = held["x"][level, rows] + exchange.take(2 * level, part, rows)
+            held["h"][level, rows] = h
+            n2 = low(h * rms_scale(h) * gain_ref[level, 1:2, :].astype(F32))
+            held["n2"][level, rows] = n2
+            if part == 0:
+                loads[level][2].wait()
+            g = dot_nn(n2, wgu[level, 0])
+            held["gu"][level, 0, rows] = g
+            u = dot_nn(n2, wgu[level, 1])
+            held["gu"][level, 1, rows] = u
+            z = low(g * sigmoid(g) * u)
+            held["z"][level, rows] = z
+            if part == 0:
+                loads[level][3].wait()
+            out = low(dot_nn(z, wd[level]))
+            if level < LAYERS - 1:
+                exchange.give(2 * level + 1, part, rows, out)
+            else:
+                last[rows] = out
+        for name in ("h", "n2", "gu", "z"):
+            keep(name, level)
+    final = pltpu.make_async_copy(last, last_out, load_sems.at[0, 0])
+    final.start()
+    for copy in keeps:
+        copy.wait()
+    final.wait()
+    exchange.finish()
+
+
+def forward(x, norm_gain, taps, head_gain, wb, wq, wo, wgu, wd):
     length, width = x.shape
-    chans = wq.shape[-1]
-    heads = chans // DK
-    sds = jax.ShapeDtypeStruct
+    chans, hidden = wq.shape[-1], wgu.shape[-1]
+    n_tensor = lax.axis_size("tensor")
+    n_parts = 2
+    kept = kept_shapes(length, width, chans, hidden)
     vmem = pl.BlockSpec(memory_space=pltpu.VMEM)
     hbm = pl.BlockSpec(memory_space=pl.ANY)
-    return pl.pallas_call(
-        functools.partial(mixer_forward_kernel, level, heads, len(adds)),
+    spots = 2 * LAYERS - 1
+    *kept, part = pl.pallas_call(
+        functools.partial(forward_kernel, n_parts),
         out_shape=(
-            sds((length, width), F32),
-            sds((length, width), BF16),
-            sds((3, length, chans), F32),
-            sds((length, LANES), F32),
-            sds((2, heads, length, length), BF16),
-            sds((length, chans), BF16),
-            sds((length, chans), F32),
-            sds((length, chans), BF16),
-            sds((length, width), BF16),
+            *(jax.ShapeDtypeStruct(*spec) for spec in kept),
+            jax.ShapeDtypeStruct((length, width), BF16),
         ),
-        in_specs=[vmem] * (5 + len(adds)) + [hbm, hbm],
-        out_specs=(vmem,) * 9,
+        in_specs=[vmem] * 5 + [hbm] * 4,
+        out_specs=(hbm,) * (len(kept) + 1),
         scratch_shapes=[
-            pltpu.VMEM((3, width, chans), BF16),
-            pltpu.VMEM((chans, width), BF16),
-            pltpu.SemaphoreType.DMA((2,)),
+            *(pltpu.VMEM(*spec) for spec in kept),
+            pltpu.VMEM((LAYERS, 3, width, chans), BF16),
+            pltpu.VMEM((LAYERS, chans, width), BF16),
+            pltpu.VMEM((LAYERS, 2, width, hidden), BF16),
+            pltpu.VMEM((LAYERS, hidden, width), BF16),
+            pltpu.VMEM((spots, n_tensor, length, width), BF16),
+            pltpu.VMEM((length, width), BF16),
+            pltpu.SemaphoreType.DMA((LAYERS, 4)),
+            pltpu.SemaphoreType.DMA((len(kept), LAYERS)),
+            pltpu.SemaphoreType.DMA((spots, n_parts, n_tensor - 1)),
+            pltpu.SemaphoreType.DMA((spots, n_parts, n_tensor - 1)),
         ],
-        compiler_params=pltpu.CompilerParams(vmem_limit_bytes=VMEM_LIMIT),
-        name="mixer_forward",
-    )(x, *adds, norm_gain, taps, head_gain, wb, wq, wo)
-
-
-def mlp_forward_kernel(level, n_add, *refs):
-    (x_ref, *adds) = refs[: 1 + n_add]
-    (gain_ref, wgu_hbm, wd_hbm) = refs[1 + n_add : 4 + n_add]
-    (h_out, n2_out, gu_out, z_out, part_out) = refs[4 + n_add : 9 + n_add]
-    wgu, wd, sems = refs[9 + n_add :]
-    loads = [
-        pltpu.make_async_copy(wgu_hbm.at[level, 0], wgu.at[0], sems.at[0]),
-        pltpu.make_async_copy(wgu_hbm.at[level, 1], wgu.at[1], sems.at[1]),
-        pltpu.make_async_copy(wd_hbm.at[level], wd, sems.at[2]),
-    ]
-    for load in loads:
-        load.start()
-    h = x_ref[...].astype(F32)
-    for add in adds:
-        h = h + add[...].astype(F32)
-    h_out[...] = h
-    n2 = low(h * rms_scale(h) * gain_ref[level, 1:2, :].astype(F32))
-    n2_out[...] = n2
-    loads[0].wait()
-    g = dot_nn(n2, wgu[0])
-    gu_out[0] = g
-    loads[1].wait()
-    u = dot_nn(n2, wgu[1])
-    gu_out[1] = u
-    z = low(g * sigmoid(g) * u)
-    z_out[...] = z
-    loads[2].wait()
-    part_out[...] = low(dot_nn(z, wd[...]))
-
-
-def mlp_forward(level, x, adds, norm_gain, wgu, wd):
-    length, width = x.shape
-    hidden = wgu.shape[-1]
-    sds = jax.ShapeDtypeStruct
-    vmem = pl.BlockSpec(memory_space=pltpu.VMEM)
-    hbm = pl.BlockSpec(memory_space=pl.ANY)
-    return pl.pallas_call(
-        functools.partial(mlp_forward_kernel, level, len(adds)),
-        out_shape=(
-            sds((length, width), F32),
-            sds((length, width), BF16),
-            sds((2, length, hidden), F32),
-            sds((length, hidden), BF16),
-            sds((length, width), BF16),
+        compiler_params=pltpu.CompilerParams(
+            vmem_limit_bytes=VMEM_LIMIT, collective_id=1, has_side_effects=True
         ),
-        in_specs=[vmem] * (2 + len(adds)) + [hbm, hbm],
-        out_specs=(vmem,) * 5,
-        scratch_shapes=[
-            pltpu.VMEM((2, width, hidden), BF16),
-            pltpu.VMEM((hidden, width), BF16),
-            pltpu.SemaphoreType.DMA((3,)),
-        ],
-        compiler_params=pltpu.CompilerParams(vmem_limit_bytes=VMEM_LIMIT),
-        name="mlp_forward",
-    )(x, *adds, norm_gain, wgu, wd)
+        name="forward",
+    )(x, norm_gain, taps, head_gain, wb, wq, wo, wgu, wd)
+    return dict(zip(KEPT, kept)), part
 
 
 def back_through_norm(level, which, gain_ref, e_ref, hid_ref, adds, rows_out):
@@ -771,19 +852,30 @@
 ):
     heads = beta_weight.shape[-1]
     wb = jnp.pad(beta_weight, ((0, 0), (0, 0), (0, LANES - heads)))
-    base, adds = inputs, ()
+    saved, part = forward(
+        inputs,
+        norm_gain,
+        conv_taps,
+        out_gain,
+        wb,
+        qkv_weight,
+        out_weight,
+        gate_up_weight,
+        down_weight,
+    )
     kept = []
     for level in range(LAYERS):
-        x, n1, p, logits, t, u, o, on, part = mixer_forward(
-            level, base, adds, norm_gain, conv_taps, out_gain, wb, qkv_weight, out_weight
-        )
-        h, n2, gu, z, part_two = mlp_forward(
-            level, x, branch_parts(part), norm_gain, gate_up_weight, down_weight
-        )
-        kept.append((x, h, (n1, p, logits, t, u, o, on), (n2, gu, z)))
-        base, adds = h, branch_parts(part_two)
-    total = base
-    for add in adds:
+        at = {name: saved[name][level] for name in KEPT}
+        kept.append(
+            (
+                at["x"],
+                at["h"],
+                tuple(at[name] for name in ("n1", "p", "logits", "t", "u", "o", "on")),
+                tuple(at[name] for name in ("n2", "gu", "z")),
+            )
+        )
+    total = kept[-1][1]
+    for add in branch_parts(part):
         total = total + add.astype(F32)
     outputs = total.astype(BF16)
 

time: 505 us -> 492 us (0.974)
  waiting for transfers between devices: 73.9 us -> 29 us
  local copies, waits for them, and re-layouts: 14.3 us -> 32.6 us
  Pallas kernels: 361 us -> 379 us
    ppermute x9 -> x6, waiting for transfers between devices: 73.9 us -> 29 us  [branch_parts(): return (part, lax.ppermute(part, 'tensor', [(0, 1), (1, 0)]))]
    squeeze x0 -> x11, local copies, waits for them, and re-layouts: none -> 20.4 us  [body(): at = {name: saved[name][level] for name in KEPT}]
    pallas_call x4 -> x1, Pallas kernels: 46.2 us -> 62.8 us  [forward(): pl.pallas_call(functools.partial(forward_kernel, n_parts), out_shape=(*(j...]
    ppermute x9 -> x6, starting transfers between devices: 12.5 us -> 9.1 us  [branch_parts(): return (part, lax.ppermute(part, 'tensor', [(0, 1), (1, 0)]))]
  transfers between devices with their start and end apart: 9 -> 6, of which waited for: 7 -> 4; matrix products, arithmetic and copies ran while one was open for 6% -> 9% of each run, Pallas kernels for 3% -> 3%
where the time goes in v3:
time: 492 us; the launch traced here: 483 us
  Pallas kernels  379 us (77%)
  local copies, waits for them, and re-layouts  32.6 us (7%)
  other arithmetic  32.3 us (7%)
  waiting for transfers between devices  29 us (6%)
  starting transfers between devices  9.1 us (2%)
    pallas_call x1, Pallas kernels, ring_sum(): pl.pallas_call(functools.partial(ring_kernel, n_dp, tuple(kinds)), out_sh...  261 us
    pallas_call x1, Pallas kernels, forward(): pl.pallas_call(functools.partial(forward_kernel, n_parts), out_shape=(*(j...  62.8 us
    ppermute x6, waiting for transfers between devices, branch_parts(): return (part, lax.ppermute(part, 'tensor', [(0, 1), (1, 0)]))  29 us
    pallas_call x2, Pallas kernels, mixer_backward(): pl.pallas_call(functools.partial(mixer_backward_kernel, level, heads, len...  29 us
    pallas_call x2, Pallas kernels, mlp_backward(): pl.pallas_call(functools.partial(mlp_backward_kernel, level, len(adds)),...  26.5 us
    convert_element_type x4, other arithmetic, body(): jnp.stack([sums[4 + index], sums[index]]).astype(F32)  25.3 us
    squeeze x11, local copies, waits for them, and re-layouts, body(): at = {name: saved[name][level] for name in KEPT}  20.4 us
  transfers between devices with their start and end apart: 6, of which 4 were waited for; matrix products, arithmetic and copies ran while one was open for 9% of the time, Pallas kernels for 3%

profile of v3, /device:TPU:0, one launch (start us, length us, event | category | flops | bytes accessed | tf_op | source)
XLA Modules:
  0.0 482.8 jit_solution(18004515427114457085)
XLA Ops:
  2.6 62.8 %forward.1 = (f32[2,256,1024]{2,1,0:T(8,128)}, bf16[2,256,1024]{2,1,0:T(8,128)(2,1)}, f32[2,3,256,512]{3,2,1,0:T(8,128)}, f32[2,256,128]{2,1,0:T(8,128)}, bf16[2...) custom-call(bf16[256,1024]{1,0:T(8,128)(2,1)} %refs_0_.2, ...), custom_call_target="tpu_custom_call" | custom-call | tf_op jit(solution)/shard_map/forward/pallas_call | solution.py:322
  65.4 2.3 slice_bitcast_fusion.7.refs_1_
  67.7 2.2 slice_bitcast_fusion.13
  70.0 5.7 %slice_bitcast_fusion = (f32[2,256,1408]{2,1,0:T(8,128)}, f32[2,256,1408]{2,1,0:T(8,128)}) fusion(f32[2,2,256,1408]{3,2,1,0:T(8,128)} %get-tuple-element.79), kind=kLoop, calls=%fused_computation.3 | loop fusion | bytes 11534336 | tf_op jit(solution)/shard_map/squeeze | solution.py:868
  75.7 1.2 slice_bitcast_fusion.9
  76.9 13.0 %mlp_backward.2 = (f32[256,1024]{1,0:T(8,128)}, f32[1,1024]{1,0:T(1,128)}, bf16[256,1024]{1,0:T(8,128)(2,1)}, bf16[1408,1024]{1,0:T(8,128)(2,1)}, bf16[2,1024,1408]{2,1,0:T(8,128)(2,1)}) custom-call(bf16[256,1024]{1,0:T(8,128)(2,1)} %refs_0_.3, f32[256,1024]{1,0:T(8,128)} %slice_bitcast_fusion.7.refs_1_, bf16[2,2,1024]{2,1,0:T(2,128)(2,1)} %refs_4_.5, ...), custom_call_target="tpu_custom_call" | custom-call | tf_op jit(solution)/shard_map/mlp_backward/pallas_call | solution.py:398
  89.9 2.2 collective-permute-start.1
  92.1 1.6 slice_bitcast_fusion.5
  93.7 1.1 slice_bitcast_fusion.12
  94.8 1.5 slice_bitcast_fusion.4
  99.1 2.0 slice_bitcast_fusion.2
  101.1 2.0 collective-permute-done.1.refs_3_
  103.9 14.4 %mixer_backward.2 = (f32[256,1024]{1,0:T(8,128)}, bf16[256,1024]{1,0:T(8,128)(2,1)}, f32[16,1024]{1,0:T(8,128)}, bf16[3,1024,512]{2,1,0:T(8,128)(2,1)}, bf16[512,1024]{1,0:T(8,128)(2,1)}) custom-call(f32[256,1024]{1,0:T(8,128)} %get-tuple-element.81.refs_0_, f32[256,1024]{1,0:T(8,128)} %get-tuple-element.135.refs_1_, ...), custom_call_target="tpu_custom_call" | custom-call | tf_op jit(solution)/shard_map/mixer_backward/pallas_call | solution.py:527
  118.3 1.8 collective-permute-start.2
  120.1 10.3 %collective-permute-done.2.refs_3_ = bf16[256,1024]{1,0:T(8,128)(2,1)S(1)} collective-permute-done((bf16[256,1024]{1,0:T(8,128)(2,1)}, bf16[256,1024]{1,0:T(8,128)(2,1)S(1)}, u32[]{:S(2)}, u32[]{:S(2)}) %collective-permute-start.2) | collective-permute-done | bytes 524320 | tf_op jit(solution)/shard_map/ppermute | solution.py:556
  131.2 13.5 %mlp_backward.3 = (f32[256,1024]{1,0:T(8,128)}, f32[1,1024]{1,0:T(1,128)}, bf16[256,1024]{1,0:T(8,128)(2,1)}, bf16[1408,1024]{1,0:T(8,128)(2,1)}, bf16[2,1024,1408]{2,1,0:T(8,128)(2,1)}) custom-call(f32[256,1024]{1,0:T(8,128)} %get-tuple-element.90.refs_0_, f32[256,1024]{1,0:T(8,128)} %slice_bitcast_fusion.7.refs_1_, ...), custom_call_target="tpu_custom_call" | custom-call | tf_op jit(solution)/shard_map/mlp_backward/pallas_call | solution.py:398
  144.7 1.5 collective-permute-start.3
  146.9 12.9 %collective-permute-done.3.refs_3_ = bf16[256,1024]{1,0:T(8,128)(2,1)S(1)} collective-permute-done((bf16[256,1024]{1,0:T(8,128)(2,1)}, bf16[256,1024]{1,0:T(8,128)(2,1)S(1)}, u32[]{:S(2)}, u32[]{:S(2)}) %collective-permute-start.3) | collective-permute-done | bytes 524320 | tf_op jit(solution)/shard_map/ppermute | solution.py:556
  160.6 14.6 %mixer_backward.3 = (f32[256,1024]{1,0:T(8,128)}, bf16[256,1024]{1,0:T(8,128)(2,1)}, f32[16,1024]{1,0:T(8,128)}, bf16[3,1024,512]{2,1,0:T(8,128)(2,1)}, bf16[512,1024]{1,0:T(8,128)(2,1)}) custom-call(f32[256,1024]{1,0:T(8,128)} %get-tuple-element.92.refs_0_, f32[256,1024]{1,0:T(8,128)} %get-tuple-element.134.refs_1_, ...), custom_call_target="tpu_custom_call" | custom-call | tf_op jit(solution)/shard_map/mixer_backward/pallas_call | solution.py:527
  175.2 1.5 collective-permute-start.4
  176.8 2.3 add_convert_fusion
  180.9 3.8 collective-permute-done.4
  184.7 1.4 fusion.7
  187.3 260.5 %ring_sum.1 = (bf16[8,2,32,1024]{3,2,1,0:T(8,128)(2,1)}, bf16[8,176,1024]{2,1,0:T(8,128)(2,1)}, bf16[8,2,192,512]{3,2,1,0:T(8,128)(2,1)}, bf16[8,2,128,1408]{3,2...) custom-call(bf16[8,2,32,1024]{3,2,1,0:T(8,128)(2,1)} %bitcast.106, ...), custom_call_target="tpu_custom_call" | custom-call | bytes 774635520 | tf_op jit(solution)/shard_map/ring_sum/pallas_call | solution.py:814
  447.8 1.5 slice_bitcast_fusion.23
  450.8 1.5 collective-permute-start.5
  452.4 8.6 %maximum_convert_fusion.1 = f32[2,3,1024,512]{3,2,1,0:T(8,128)} fusion(bf16[1,3,1024,512]{3,2,1,0:T(8,128)(2,1)} %bitcast.100, bf16[1,3,1024,512]{3,2,1,0:T(8,128)(2,1)} %bitcast.101), kind=kLoop, calls=%fused_computation.1 | loop fusion | flops 6291456 | bytes 18874368 | tf_op jit(solution)/shard_map/convert_element_type | solution.py:939
  460.9 2.4 maximum_convert_fusion.3
  463.4 1.7 copy-done.1
  465.1 9.2 %maximum_convert_fusion = f32[2,2,1024,1408]{3,2,1,0:T(8,128)} fusion(bf16[1,2,1024,1408]{3,2,1,0:T(8,128)(2,1)S(1)} %bitcast.96, bf16[1,2,1024,1408]{3,2,1,0:T(8,128)(2,1)S(1)} %bitcast.97), kind=kLoop, calls=%fused_computation | loop fusion | flops 11534336 | bytes 34603008 | tf_op jit(solution)/shard_map/convert_element_type | solution.py:939
  474.3 5.2 %maximum_convert_fusion.2 = f32[2,1408,1024]{2,1,0:T(8,128)} fusion(bf16[1,1408,1024]{2,1,0:T(8,128)(2,1)S(1)} %bitcast.104, bf16[1,1408,1024]{2,1,0:T(8,128)(2,1)S(1)} %bitcast.105), kind=kLoop, calls=%fused_computation.2 | loop fusion | flops 5767168 | bytes 17301504 | tf_op jit(solution)/shard_map/convert_element_type | solution.py:939
  479.5 1.2 fusion.4
  (82 shorter events, 14.4 us)
Async XLA Ops:
  70.0 5.7 %copy-start.9 = (bf16[2,256,1408]{2,1,0:T(8,128)(2,1)S(1)}, bf16[2,256,1408]{2,1,0:T(8,128)(2,1)}, u32[]{:S(2)}) copy-start(bf16[2,256,1408]{2,1,0:T(8,128)(2,1)} %get-tuple-element.80) | copy-start | bytes 4325380
  76.9 15.3 %copy-start.3 = (f32[2,256,1024]{2,1,0:T(8,128)S(1)}, f32[2,256,1024]{2,1,0:T(8,128)}, u32[]{:S(2)}) copy-start(f32[2,256,1024]{2,1,0:T(8,128)} %get-tuple-element.75) | copy-start | bytes 6291460
  89.9 3.8 copy-start.12
  89.9 13.2 %collective-permute-start.1 = (bf16[256,1024]{1,0:T(8,128)(2,1)}, bf16[256,1024]{1,0:T(8,128)(2,1)S(1)}, u32[]{:S(2)}, u32[]{:S(2)}) collective-permute-start(bf16[256,1024]{1,0:T(8,128)(2,1)} %get-tuple-element.82.refs_2_), channel_id=1, source_target_pairs={{0,1},{1,0},{2,3},{3,2},{4,5},{5,4},{6,7},{7,6},{8,9},{9,8},{10,11... | collective-permute-start | bytes 1572872 | tf_op jit(solution)/shard_map/ppermute | solution.py:556
  92.1 2.7 copy-start.7
  93.7 2.6 copy-start.11
  94.8 2.6 copy-start.19
  94.8 2.6 copy-start.20
  96.3 2.1 copy-start.21
  96.3 2.8 copy-start.4
  103.1 0.8 copy-start.16
  118.3 12.1 %collective-permute-start.2 = (bf16[256,1024]{1,0:T(8,128)(2,1)}, bf16[256,1024]{1,0:T(8,128)(2,1)S(1)}, u32[]{:S(2)}, u32[]{:S(2)}) collective-permute-start(bf16[256,1024]{1,0:T(8,128)(2,1)} %get-tuple-element.91.refs_2_), channel_id=1, source_target_pairs={{0,1},{1,0},{2,3},{3,2},{4,5},{5,4},{6,7},{7,6},{8,9},{9,8},{10,11... | collective-permute-start | bytes 1572872 | tf_op jit(solution)/shard_map/ppermute | solution.py:556
  130.4 0.8 copy-start.18
  131.2 15.0 %copy-start.15 = (bf16[256,1024]{1,0:T(8,128)(2,1)S(1)}, bf16[256,1024]{1,0:T(8,128)(2,1)}, u32[]{:S(2)}) copy-start(bf16[256,1024]{1,0:T(8,128)(2,1)} %get-tuple-element.76) | copy-start | bytes 1572868
  131.2 15.6 %copy-start = (f32[2,256,1024]{2,1,0:T(8,128)S(1)}, f32[2,256,1024]{2,1,0:T(8,128)}, u32[]{:S(2)}) copy-start(f32[2,256,1024]{2,1,0:T(8,128)} %get-tuple-element.77) | copy-start | bytes 6291460
  144.7 15.1 %collective-permute-start.3 = (bf16[256,1024]{1,0:T(8,128)(2,1)}, bf16[256,1024]{1,0:T(8,128)(2,1)S(1)}, u32[]{:S(2)}, u32[]{:S(2)}) collective-permute-start(bf16[256,1024]{1,0:T(8,128)(2,1)} %get-tuple-element.93.refs_2_), channel_id=1, source_target_pairs={{0,1},{1,0},{2,3},{3,2},{4,5},{5,4},{6,7},{7,6},{8,9},{9,8},{10,11... | collective-permute-start | bytes 1572872 | tf_op jit(solution)/shard_map/ppermute | solution.py:556
  146.2 30.6 %collective-permute-start = (bf16[256,1024]{1,0:T(8,128)(2,1)S(1)}, bf16[256,1024]{1,0:T(8,128)(2,1)S(1)}, u32[]{:S(2)}, u32[]{:S(2)}) collective-permute-start(bf16[256,1024]{1,0:T(8,128)(2,1)S(1)} %copy-done.15), channel_id=1, source_target_pairs={{0,1},{1,0},{2,3},{3,2},{4,5},{5,4},{6,7},{7,6},{8,9},{9,8},{10,11... | collective-permute-start | bytes 1572872 | tf_op jit(solution)/shard_map/ppermute | solution.py:556
  160.6 16.2 %copy-start.22 = (bf16[2,2,1024]{2,1,0:T(2,128)(2,1)S(1)}, bf16[2,2,1024]{2,1,0:T(2,128)(2,1)}, u32[]{:S(2)}) copy-start(bf16[2,2,1024]{2,1,0:T(2,128)(2,1)} %refs_4_.5) | copy-start | bytes 24580
  160.6 18.9 %copy-start.26 = (f32[1,1024]{1,0:T(1,128)S(1)}, f32[1,1024]{1,0:T(1,128)}, u32[]{:S(2)}) copy-start(f32[1,1024]{1,0:T(1,128)} %get-tuple-element.106) | copy-start | bytes 12292
  160.6 19.6 %copy-start.24 = (f32[16,1024]{1,0:T(8,128)S(1)}, f32[16,1024]{1,0:T(8,128)}, u32[]{:S(2)}) copy-start(f32[16,1024]{1,0:T(8,128)} %get-tuple-element.105) | copy-start | bytes 196612
  175.2 10.9 %copy-start.25 = (f32[16,1024]{1,0:T(8,128)S(1)}, f32[16,1024]{1,0:T(8,128)}, u32[]{:S(2)}) copy-start(f32[16,1024]{1,0:T(8,128)} %get-tuple-element.104) | copy-start | bytes 196612
  175.2 9.5 %collective-permute-start.4 = (bf16[256,1024]{1,0:T(8,128)(2,1)}, bf16[256,1024]{1,0:T(8,128)(2,1)S(1)}, u32[]{:S(2)}, u32[]{:S(2)}) collective-permute-start(bf16[256,1024]{1,0:T(8,128)(2,1)} %get-tuple-element.95), channel_id=1, source_target_pairs={{0,1},{1,0},{2,3},{3,2},{4,5},{5,4},{6,7},{7,6},{8,9},{9,8},{10,11... | collective-permute-start | bytes 1572872 | tf_op jit(solution)/shard_map/ppermute | solution.py:556
  450.8 31.2 %collective-permute-start.5 = (f32[2,128]{1,0:T(2,128)S(1)}, f32[2,128]{1,0:T(2,128)S(1)}, u32[]{:S(2)}, u32[]{:S(2)}) collective-permute-start(f32[2,128]{1,0:T(2,128)S(1)} %bitcast.118), channel_id=1, source_target_pairs={{0,1},{1,0},{2,3},{3,2},{4,5},{5,4},{6,7},{7,6},{8,9},{9,8},{10,11... | collective-permute-start | bytes 3080 | tf_op jit(solution)/shard_map/ppermute | solution.py:556
  452.3 8.6 %copy-start.13 = (bf16[8,2,32,1024]{3,2,1,0:T(8,128)(2,1)S(1)}, bf16[8,2,32,1024]{3,2,1,0:T(8,128)(2,1)}, u32[]{:S(2)}) copy-start(bf16[8,2,32,1024]{3,2,1,0:T(8,128)(2,1)} %get-tuple-element.111) | copy-start | bytes 3145732
  452.3 8.6 %copy-start.14 = (bf16[8,2,32,1024]{3,2,1,0:T(8,128)(2,1)S(1)}, bf16[8,2,32,1024]{3,2,1,0:T(8,128)(2,1)}, u32[]{:S(2)}) copy-start(bf16[8,2,32,1024]{3,2,1,0:T(8,128)(2,1)} %get-tuple-element.110) | copy-start | bytes 3145732
  452.4 11.0 %copy-start.2 = (bf16[8,2,128,1408]{3,2,1,0:T(8,128)(2,1)S(1)}, bf16[8,2,128,1408]{3,2,1,0:T(8,128)(2,1)}, u32[]{:S(2)}) copy-start(bf16[8,2,128,1408]{3,2,1,0:T(8,128)(2,1)} %get-tuple-element.112) | copy-start | bytes 17301508
  460.9 4.2 copy-start.1
  465.1 9.2 %copy-start.5 = (bf16[8,176,1024]{2,1,0:T(8,128)(2,1)S(1)}, bf16[8,176,1024]{2,1,0:T(8,128)(2,1)}, u32[]{:S(2)}) copy-start(bf16[8,176,1024]{2,1,0:T(8,128)(2,1)} %get-tuple-element.115) | copy-start | bytes 8650756
  465.1 9.2 %copy-start.6 = (bf16[8,176,1024]{2,1,0:T(8,128)(2,1)S(1)}, bf16[8,176,1024]{2,1,0:T(8,128)(2,1)}, u32[]{:S(2)}) copy-start(bf16[8,176,1024]{2,1,0:T(8,128)(2,1)} %get-tuple-element.114) | copy-start | bytes 8650756
  474.3 5.2 %copy-start.8 = (bf16[256,1024]{1,0:T(8,128)(2,1)S(1)}, bf16[256,1024]{1,0:T(8,128)(2,1)}, u32[]{:S(2)}) copy-start(bf16[256,1024]{1,0:T(8,128)(2,1)} %get-tuple-element.95) | copy-start | bytes 1572868
  474.3 5.2 %copy-start.10 = (f32[256,1024]{1,0:T(8,128)S(1)}, f32[256,1024]{1,0:T(8,128)}, u32[]{:S(2)}) copy-start(f32[256,1024]{1,0:T(8,128)} %get-tuple-element.94) | copy-start | bytes 3145732
  479.5 1.2 copy-start.23
  (1 other events, 0.8 us)
